TPU v7x, 128 devices: a whole 4x4x4 slice. The times are simulated.
128 devices in a mesh: req: 16 (over y, x), head: 8 (over z, core).
Axes of the slice: x: 4, y: 4, z: 4, core: 2. Of those that a mesh axis runs over, the one named last changes fastest.
Arguments:
- hidden_in: bfloat16 [8192, 2048], P(('req', 'head')), may hold values from -6 to 6
- segment_ids: int32 [16, 512], P('req', 'head'), may hold values from 0 to 3, never falling along the last dimension, each value on 1 to 256 neighbouring positions
- attn_routes: int32 [8192, 2], P(('req', 'head')), may hold values from 0 to 7, all different within a row; in each aligned block of 512 rows (0 to 511, 512 to 1023, ...) at most 192 rows name the same one
- ffn_routes: int32 [8192, 2], P(('req', 'head')), may hold values from 0 to 7, all different within a row; in each aligned block of 64 rows (0 to 63, 64 to 127, ...) at most 24 rows name the same one
- attn_gain: float32 [2048], replicated, may hold values from 0.1 to 1.9
- attn_router: float32 [2048, 8], replicated, may hold values from -0.125 to 0.125
- w_query: bfloat16 [8, 2048, 2048], P(None, None, 'head'), may hold values from -1 to 1
- w_key: bfloat16 [2048, 2048], P(None, 'head'), may hold values from -32 to 32
- w_value: bfloat16 [2048, 2048], P(None, 'head'), may hold values from -0.125 to 0.125
- w_out: bfloat16 [8, 2048, 2048], P(None, 'head'), may hold values from -0.125 to 0.125
- ffn_gain: float32 [2048], replicated, may hold values from 0.1 to 1.9
- ffn_router: float32 [2048, 8], replicated, may hold values from -0.125 to 0.125
- w_gate_up: bfloat16 [8, 2048, 2, 5632], P('head', None, None, 'req'), may hold values from -0.125 to 0.125
- w_down: bfloat16 [8, 5632, 2048], P('head', 'req'), may hold values from -0.078125 to 0.078125
Outputs:
- layer_out: bfloat16 [8192, 2048], P(('req', 'head'))
Inputs may be any that keep to these rules, and one draw needn't show every extreme that they name: `segment_ids`: within each row segment numbers never fall; each segment has 1 to 256 tokens. `attn_routes`: each token names two different experts; in each aligned block of 512 rows no expert is named by more than 192 rows. `ffn_routes`: each token names two different experts; in each aligned block of 64 rows (the rows of one device) no expert is named by more than 24 rows.
All inputs are finite; a program needn't handle non-finite values.
Results may differ from a plain program's by a relative error of at most 0.015.
Values may be sent and summed in bfloat16 or wider, within the bound.
No kernel may reach another device: no remote copies, remote signals or barrier semaphores. Data moves between devices by JAX's collectives and lax.ppermute only.
A program may use at most 128 MiB of HBM per device.

v0:
```python
import jax
import jax.numpy as jnp
from jax import lax
from jax.experimental import pallas as pl
from jax.experimental.pallas import tpu as pltpu
from jax.sharding import PartitionSpec as P


D = 2048
HD = 128
META = 128
ROWS = 64
SEQ = 512
SLOTS = 24
HID = 352
FF4 = 4 * HID
BF = jnp.bfloat16
F32 = jnp.float32
EPSILON = 1e-06
ROPE_BASE = 10000.0
AXES = ("req", "head")


def mate(v, parity):
    return v ^ 1 if parity == 0 else ((((v - 1) % 4) ^ 1) + 1) % 4


def square_perm(move_x, move_y, flip):
    pairs = []
    for i in range(128):
        r, h = divmod(i, 8)
        y, x = divmod(r, 4)
        parity = (h & 1) ^ flip
        ny = mate(y, parity) if move_y else y
        nx = mate(x, parity) if move_x else x
        pairs.append((i, (ny * 4 + nx) * 8 + h))
    return pairs


WX, WY = square_perm(1, 0, 0), square_perm(0, 1, 0)
TX, TY, TXY = square_perm(1, 0, 1), square_perm(0, 1, 1), square_perm(1, 1, 1)
HA = [(h, h ^ (6 if h & 1 else 2)) for h in range(8)]
HB = [(h, h ^ (2 if h & 1 else 6)) for h in range(8)]
HC = [(h, h ^ 1) for h in range(8)]


def send_xy(v, pairs):
    return lax.ppermute(v, AXES, pairs)


def send_h(v, pairs):
    return lax.ppermute(v, "head", pairs)


def gather_head(own):
    a1 = send_h(own, HA)
    b1 = send_h(own, HB)
    c0 = send_h(own, HC)
    b2 = send_h(a1, HB)
    c1 = send_h(a1, HC)
    c2 = send_h(b1, HC)
    c3 = send_h(b2, HC)
    return [own, a1, b1, b2, c0, c1, c2, c3]


def head_order(scatter):
    h = lax.axis_index("head")
    m_a = 2 + 4 * (h & 1)
    m_b = 8 - m_a
    if scatter:
        m_a, m_b = m_b, m_a
        masks = (0, m_a, m_b, 4, 1, m_b ^ 1, m_a ^ 1, 5)
    else:
        masks = (0, m_a, m_b, 4, 1, m_b ^ 1, m_a ^ 1, 5)
    return [h ^ m for m in masks]


def split_router(router):
    hi = router.astype(BF).astype(F32)
    mid = (router - hi).astype(BF).astype(F32)
    low = router - hi - mid
    return jnp.concatenate([hi, mid, low, jnp.zeros_like(low)], axis=0).astype(BF)


def normalize(chunk, gain):
    wide = chunk.astype(F32)
    inverse = lax.rsqrt(jnp.mean(wide * wide, axis=-1, keepdims=True) + EPSILON)
    return (wide * inverse * gain).astype(BF)


def picked_gates(logits3, first, second):
    lane = lax.broadcasted_iota(jnp.int32, logits3.shape, 1)
    expert = (lane & 7).astype(F32)
    diff = jnp.where(expert == first, logits3, 0.0) - jnp.where(expert == second, logits3, 0.0)
    delta = jnp.sum(diff, axis=1, keepdims=True)
    return 1.0 / (1.0 + jnp.exp(-delta)), 1.0 / (1.0 + jnp.exp(delta))


def matmul(a, b):
    return jnp.dot(a, b, preferred_element_type=F32)


def matmul_t(a, b):
    return lax.dot_general(a, b, (((1,), (1,)), ((), ())), preferred_element_type=F32)


def attention_body(
    c0, c1, c2, c3, c4, c5, c6, c7,
    gain, router, cos_t, sin_t, wq, wk, wv, wo,
    keep, send,
    x_s, meta_s, q_s, k_s, v_s, rope_c, rope_s, gate_s, ctx_s, mix_s,
):
    step = pl.program_id(0)

    @pl.when(step == 0)
    def _():
        for place, ref in zip(head_order(False), (c0, c1, c2, c3, c4, c5, c6, c7)):
            base = pl.multiple_of(place * ROWS, ROWS)
            x_s[pl.ds(base, ROWS), :] = normalize(ref[:, :D], gain[...])
            meta_s[pl.ds(base, ROWS), :] = ref[:, D:].astype(F32)
        seg = meta_s[:, 0:1]
        cos_all = cos_t[...]
        sin_all = sin_t[...]
        c_sel = jnp.broadcast_to(cos_t[0:1, :], (SEQ, HD))
        s_sel = jnp.broadcast_to(sin_t[0:1, :], (SEQ, HD))
        for number in (1, 2, 3):
            start = jnp.sum(jnp.where(seg < float(number), 1.0, 0.0)).astype(jnp.int32)
            start = jnp.minimum(start, SEQ - 1)
            here = seg == float(number)
            c_sel = jnp.where(here, cos_t[pl.ds(start, 1), :], c_sel)
            s_sel = jnp.where(here, sin_t[pl.ds(start, 1), :], s_sel)
        lane = lax.broadcasted_iota(jnp.int32, (SEQ, HD), 1)
        rope_c[...] = cos_all * c_sel + sin_all * s_sel
        turned = sin_all * c_sel - cos_all * s_sel
        rope_s[...] = jnp.where(lane < HD // 2, -turned, turned)
        x = x_s[...]
        keys = matmul(x, wk[...])
        for g in range(2):
            one = keys[:, g * HD : (g + 1) * HD]
            k_s[:, g * HD : (g + 1) * HD] = (
                one * rope_c[...] + pltpu.roll(one, HD // 2, 1) * rope_s[...]
            ).astype(BF)
        v_s[...] = matmul(x, wv[...]).astype(BF)
        logits3 = matmul_t(x, split_router(router[...]))
        g0, g1 = picked_gates(logits3, meta_s[:, 1:2], meta_s[:, 2:3])
        gate_s[:, 0:1] = g0
        gate_s[:, 1:2] = g1

    @pl.when(step < 8)
    def _():
        here = step.astype(F32)
        query = matmul(x_s[...], wq[0])
        for j in range(2):
            chosen = meta_s[:, 1 + j : 2 + j] == here
            q_s[j] = jnp.where(chosen, query, q_s[j])

    @pl.when(step == 7)
    def _():
        seg_row = jnp.transpose(meta_s[...])[0:1, :]
        for g in range(2):
            cols = slice(g * HD, (g + 1) * HD)
            for block in range(4):
                lo = max(0, block * 128 - 256)
                hi = block * 128 + 128
                rows = slice(block * 128, hi)
                parts = []
                for j in range(2):
                    one = q_s[j, rows, cols]
                    parts.append(
                        (one * rope_c[rows, :] + pltpu.roll(one, HD // 2, 1) * rope_s[rows, :]).astype(BF)
                    )
                query = jnp.concatenate(parts, axis=0)
                scores = matmul_t(query, k_s[lo:hi, cols]) * HD ** (-0.5)
                q_pos = lax.broadcasted_iota(jnp.int32, (128, hi - lo), 0) + block * 128
                k_pos = lax.broadcasted_iota(jnp.int32, (128, hi - lo), 1) + lo
                allowed = (meta_s[rows, 0:1] == seg_row[:, lo:hi]) & (k_pos <= q_pos)
                allowed = jnp.concatenate([allowed.astype(F32)] * 2, axis=0) > 0.5
                masked = jnp.where(allowed, scores, -1e30)
                largest = jnp.max(masked, axis=-1, keepdims=True)
                exponent = jnp.exp(masked - largest)
                total = jnp.sum(exponent, axis=-1, keepdims=True)
                probs = (exponent / total).astype(BF)
                context = matmul(probs, v_s[lo:hi, cols])
                ctx_s[0, rows, cols] = context[:128]
                ctx_s[1, rows, cols] = context[128:]
        for i, place in enumerate(head_order(True)):
            base = pl.multiple_of(place * ROWS, ROWS)
            take = pl.ds(base, ROWS)
            first = ctx_s[0, take, :].astype(BF).astype(F32) * gate_s[take, 0:1]
            second = ctx_s[1, take, :].astype(BF).astype(F32) * gate_s[take, 1:2]
            meta = meta_s[take, :]
            for e in range(8):
                mixed = jnp.where(meta[:, 1:2] == float(e), first, 0.0) + jnp.where(
                    meta[:, 2:3] == float(e), second, 0.0
                )
                mix_s[i * ROWS : (i + 1) * ROWS, e * 256 : (e + 1) * 256] = mixed.astype(BF)

    @pl.when(step >= 8)
    def _():
        weights = wo[...].reshape(8 * 256, 512)
        out = matmul(mix_s[...], weights)
        keep[...] = out[:256].astype(BF)
        send[...] = out[256:].astype(BF)


def attention(chunks, gain, router, cos_t, sin_t, w_query, w_key, w_value, w_out):
    whole = lambda shape: pl.BlockSpec(shape, lambda i: (0,) * len(shape))
    spec = pltpu.PrefetchScalarGridSpec(
        num_scalar_prefetch=0,
        grid=(12,),
        in_specs=[whole((ROWS, D + META))] * 8
        + [
            whole((1, D)),
            whole((8, D)),
            whole((SEQ, HD)),
            whole((SEQ, HD)),
            pl.BlockSpec((1, D, 256), lambda i: (jnp.minimum(i, 7), 0, 0)),
            whole((D, 256)),
            whole((D, 256)),
            pl.BlockSpec((8, 256, 512), lambda i: (0, 0, jnp.maximum(i - 8, 0))),
        ],
        out_specs=[
            pl.BlockSpec((256, 512), lambda i: (0, jnp.maximum(i - 8, 0))),
            pl.BlockSpec((256, 512), lambda i: (0, jnp.maximum(i - 8, 0))),
        ],
        scratch_shapes=[
            pltpu.VMEM((SEQ, D), BF),
            pltpu.VMEM((SEQ, META), F32),
            pltpu.VMEM((2, SEQ, 256), F32),
            pltpu.VMEM((SEQ, 256), BF),
            pltpu.VMEM((SEQ, 256), BF),
            pltpu.VMEM((SEQ, HD), F32),
            pltpu.VMEM((SEQ, HD), F32),
            pltpu.VMEM((SEQ, META), F32),
            pltpu.VMEM((2, SEQ, 256), F32),
            pltpu.VMEM((SEQ, 8 * 256), BF),
        ],
    )
    return pl.pallas_call(
        attention_body,
        grid_spec=spec,
        out_shape=[
            jax.ShapeDtypeStruct((256, D), BF),
            jax.ShapeDtypeStruct((256, D), BF),
        ],
        compiler_params=pltpu.CompilerParams(vmem_limit_bytes=40 << 20),
        name="attention",
    )(*chunks, gain, router, cos_t, sin_t, w_query, w_key, w_value, w_out)


def prepare_body(hidden, segments, routes, out):
    out[:, :D] = hidden[...]
    rows = jnp.concatenate([segments[...], routes[...], jnp.zeros((5, ROWS), jnp.int32)], axis=0).astype(F32)
    rows = jnp.concatenate([rows, jnp.zeros((META - 8, ROWS), F32)], axis=0)
    out[:, D:] = jnp.transpose(rows).astype(BF)


def prepare(hidden, segments, routes):
    vmem = pl.BlockSpec(memory_space=pltpu.VMEM)
    return pl.pallas_call(
        prepare_body,
        in_specs=[vmem] * 3,
        out_specs=vmem,
        out_shape=jax.ShapeDtypeStruct((ROWS, D + META), BF),
        compiler_params=pltpu.CompilerParams(vmem_limit_bytes=8 << 20),
        name="prepare",
    )(hidden, segments, routes)


def slot_rows(routes):
    first = routes[0:1, :]
    second = routes[1:2, :]
    expert = lax.broadcasted_iota(jnp.int32, (16, ROWS), 0)
    named = jnp.where((expert == first) | (expert == second), 1.0, 0.0)
    src = lax.broadcasted_iota(jnp.int32, (ROWS, ROWS), 0)
    dst = lax.broadcasted_iota(jnp.int32, (ROWS, ROWS), 1)
    rank = matmul(named.astype(BF), jnp.where(src < dst, 1.0, 0.0).astype(BF)).astype(jnp.int32)
    rank0 = jnp.sum(jnp.where(expert == first, rank, 0), axis=0, keepdims=True)
    rank1 = jnp.sum(jnp.where(expert == second, rank, 0), axis=0, keepdims=True)
    return first * SLOTS + rank0, second * SLOTS + rank1


def settle_body(hidden, keep, got, got_a, got_b, gain, routes, residual, rows):
    total = keep[:ROWS].astype(F32) + got[:ROWS].astype(F32) + got_a[:ROWS].astype(F32) + got_b[...].astype(F32)
    value = (hidden[...].astype(F32) + total).astype(BF)
    residual[...] = value
    normed = normalize(value, gain[...])
    slot0, slot1 = slot_rows(routes[...])
    row = lax.broadcasted_iota(jnp.int32, (8 * SLOTS, ROWS), 0)
    pick = jnp.where((row == slot0) | (row == slot1), 1.0, 0.0).astype(BF)
    rows[...] = matmul(pick, normed).astype(BF)


def settle(hidden, keep, got, got_a, got_b, gain, routes):
    vmem = pl.BlockSpec(memory_space=pltpu.VMEM)
    part = lambda n: pl.BlockSpec((n, D), lambda i: (0, 0))
    full = lambda shape: pl.BlockSpec(shape, lambda i: (0, 0))
    return pl.pallas_call(
        settle_body,
        grid=(1,),
        in_specs=[part(ROWS)] * 5 + [full((1, D)), full((2, ROWS))],
        out_specs=[part(ROWS), part(8 * SLOTS)],
        out_shape=[jax.ShapeDtypeStruct((ROWS, D), BF), jax.ShapeDtypeStruct((8 * SLOTS, D), BF)],
        compiler_params=pltpu.CompilerParams(vmem_limit_bytes=8 << 20),
        name="settle",
    )(hidden, keep, got, got_a, got_b, gain, routes)


def weigh_body(residual, gain, router, routes, high, low):
    normed = normalize(residual[...], gain[...])
    split = matmul_t(split_router(router[...]), normed)
    logits = split[0:8] + split[8:16] + split[16:24]
    expert = lax.broadcasted_iota(jnp.int32, (8, ROWS), 0)
    picked = routes[...]
    one = jnp.sum(jnp.where(expert == picked[0:1], logits, 0.0), axis=0, keepdims=True)
    two = jnp.sum(jnp.where(expert == picked[1:2], logits, 0.0), axis=0, keepdims=True)
    slot0, slot1 = slot_rows(picked)
    row = lax.broadcasted_iota(jnp.int32, (8 * SLOTS, ROWS), 0)
    table = jnp.where(row == slot0, 1.0 / (1.0 + jnp.exp(two - one)), 0.0) + jnp.where(
        row == slot1, 1.0 / (1.0 + jnp.exp(one - two)), 0.0
    )
    top = table.astype(BF)
    high[...] = top
    low[...] = (table - top.astype(F32)).astype(BF)


def weigh(residual, gain, router, routes):
    vmem = pl.BlockSpec(memory_space=pltpu.VMEM)
    return pl.pallas_call(
        weigh_body,
        in_specs=[vmem] * 4,
        out_specs=[vmem, vmem],
        out_shape=[jax.ShapeDtypeStruct((8 * SLOTS, ROWS), BF)] * 2,
        compiler_params=pltpu.CompilerParams(vmem_limit_bytes=8 << 20),
        name="weigh",
    )(residual, gain, router, routes)


def finish_body(residual, high, low, rows, out):
    values = rows[...]
    first_dim = (((0,), (0,)), ((), ()))
    mixture = lax.dot_general(high[...], values, first_dim, preferred_element_type=F32)
    mixture = mixture + lax.dot_general(low[...], values, first_dim, preferred_element_type=F32)
    out[...] = (residual[...].astype(F32) + mixture).astype(BF)


def finish(residual, high, low, rows):
    vmem = pl.BlockSpec(memory_space=pltpu.VMEM)
    return pl.pallas_call(
        finish_body,
        in_specs=[vmem] * 4,
        out_specs=vmem,
        out_shape=jax.ShapeDtypeStruct((ROWS, D), BF),
        compiler_params=pltpu.CompilerParams(vmem_limit_bytes=8 << 20),
        name="finish",
    )(residual, high, low, rows)


def pack_body(*refs):
    out, sems = refs[8], refs[9]
    copies = []
    for s in range(4):
        for part in range(3):
            src = refs[s].at[part] if part < 2 else refs[4 + s]
            place = pl.ds(part * FF4 + s * HID, HID)
            copies.append(pltpu.make_async_copy(src, out.at[place, :], sems.at[part, s]))
    for copy in copies:
        copy.start()
    for copy in copies:
        copy.wait()


def pack(gus, downs):
    hbm = pl.BlockSpec(memory_space=pl.ANY)
    return pl.pallas_call(
        pack_body,
        in_specs=[hbm] * 8,
        out_specs=pl.BlockSpec(memory_space=pltpu.VMEM),
        out_shape=pltpu.VMEM((3 * FF4, D), BF),
        scratch_shapes=[pltpu.SemaphoreType.DMA((3, 4))],
        compiler_params=pltpu.CompilerParams(vmem_limit_bytes=4 << 20),
        name="pack",
    )(*gus, *downs)


def expert_body(rows, weights, out, act_s):
    x = rows[...]
    for lo in range(0, FF4, 256):
        hi = min(lo + 256, FF4)
        gate = matmul_t(x, weights[lo:hi, :])
        up = matmul_t(x, weights[FF4 + lo : FF4 + hi, :])
        act_s[:, lo:hi] = (gate / (1.0 + jnp.exp(-gate)) * up).astype(BF)
    act = act_s[...]
    for lo in range(0, D, 256):
        out[:, lo : lo + 256] = matmul(act, weights[2 * FF4 :, lo : lo + 256]).astype(BF)


def experts(rows, weights):
    vmem = pl.BlockSpec(memory_space=pltpu.VMEM)
    return pl.pallas_call(
        expert_body,
        in_specs=[vmem] * 2,
        out_specs=vmem,
        out_shape=jax.ShapeDtypeStruct(rows.shape, BF),
        scratch_shapes=[pltpu.VMEM((rows.shape[0], FF4), BF)],
        compiler_params=pltpu.CompilerParams(vmem_limit_bytes=8 << 20),
    )(rows, weights)


def per_device(
    hidden_in,
    segment_ids,
    attn_routes,
    ffn_routes,
    attn_gain,
    attn_router,
    w_query,
    w_key,
    w_value,
    w_out,
    ffn_gain,
    ffn_router,
    w_gate_up,
    w_down,
):
    gu = jnp.transpose(w_gate_up[0], (1, 2, 0))
    down = w_down[0]
    own = prepare(hidden_in, segment_ids, attn_routes.T)
    chunks = gather_head(own)
    gu_x = send_xy(gu, WX)
    down_y = send_xy(down, WY)
    gu_y = send_xy(gu, WY)
    down_x = send_xy(down, WX)
    gu_d = send_xy(gu_x, WY)
    down_d = send_xy(down_y, WX)

    half = HD // 2
    inverse = ROPE_BASE ** (-jnp.arange(half, dtype=F32) / half)
    angles = jnp.arange(SEQ, dtype=F32)[:, None] * jnp.concatenate([inverse, inverse])[None, :]
    cosine, sine = jnp.cos(angles), jnp.sin(angles)
    keep, send = attention(
        chunks, attn_gain[None, :], attn_router.T, cosine, sine, w_query, w_key, w_value, w_out
    )
    got = send_h(send, HC)
    pass_a = (keep[128:].astype(F32) + got[128:].astype(F32)).astype(BF)
    got_a = send_h(pass_a, HA)
    held = keep[64:128].astype(F32) + got[64:128].astype(F32) + got_a[64:].astype(F32)
    got_b = send_h(held.astype(BF), HB)
    residual, rows = settle(hidden_in, keep, got, got_a, got_b, ffn_gain[None, :], ffn_routes.T)
    arrived = lax.all_to_all(rows.reshape(8, SLOTS, D), "head", split_axis=0, concat_axis=0, tiled=True)
    high, low = weigh(residual, ffn_gain[None, :], ffn_router.T, ffn_routes.T)
    x_own = arrived.reshape(8 * SLOTS, D)
    weights = pack((gu, gu_x, gu_y, gu_d), (down, down_x, down_y, down_d))
    x_d = send_xy(x_own, TXY)
    x_x = send_xy(x_own, TX)
    x_y = send_xy(x_own, TY)
    part = experts(x_own, weights)
    part_d = experts(x_d, weights)
    got_d = send_xy(part_d, TXY)
    part_x = experts(x_x, weights)
    got_x = send_xy(part_x, TX)
    part_y = experts(x_y, weights)
    got_y = send_xy(part_y, TY)
    rows = part.astype(F32) + got_d.astype(F32) + got_x.astype(F32) + got_y.astype(F32)
    rows = rows.astype(BF).reshape(8, SLOTS, D)
    returned = lax.all_to_all(rows, "head", split_axis=0, concat_axis=0, tiled=True)
    return finish(residual, high, low, returned.reshape(8 * SLOTS, D))


def solution(mesh):
    return jax.shard_map(
        per_device,
        mesh=mesh,
        in_specs=(
            P(("req", "head"), None),
            P("req", "head"),
            P(("req", "head"), None),
            P(("req", "head"), None),
            P(),
            P(),
            P(None, None, "head"),
            P(None, "head"),
            P(None, "head"),
            P(None, "head", None),
            P(),
            P(),
            P("head", None, None, "req"),
            P("head", "req", None),
        ),
        out_specs=P(("req", "head"), None),
        check_vma=False,
    )
```

profile of v0, /device:TPU:1, one launch (start us, length us, event | category | flops | bytes accessed | tf_op | source)
XLA Modules:
  0.0 207.7 jit_solution(7393273209333356999)
XLA Ops:
  0.0 3.3 %collective-permute-start.10 = (bf16[2,352,2048]{2,1,0:T(8,128)(2,1)}, bf16[2,352,2048]{2,1,0:T(8,128)(2,1)S(1)}, u32[]{:S(2)}, u32[]{:S(2)}) collective-permute-start(bf16[2,352,2048]{2,1,0:T(8,128)(2,1)} %bitcast.19), channel_id=1, source_target_pairs={{0,8},{1,25},{2,10},{3,27},{4,12},{5,29},{6,14},{7,31},{8,0},{9,17... | collective-permute-start | bytes 8650760 | tf_op jit(solution)/shard_map/ppermute | solution.py:48
  3.3 0.9 copy-done.4
  4.3 0.7 copy-done.11
  4.9 0.7 copy-done.12
  5.6 0.1 prepare.1.c0
  5.7 3.8 %collective-permute-start = (bf16[64,2176]{1,0:T(8,128)(2,1)S(1)}, bf16[64,2176]{1,0:T(8,128)(2,1)S(1)}, u32[]{:S(2)}, u32[]{:S(2)}) collective-permute-start(bf16[64,2176]{1,0:T(8,128)(2,1)S(1)} %prepare.1.c0), channel_id=1, source_target_pairs={{0,2},{1,7},{2,0},{3,5},{4,6},{5,3},{6,4},{7,1},{8,10},{9,15},{10,... | collective-permute-start | bytes 835592 | tf_op jit(solution)/shard_map/ppermute | solution.py:52
  9.5 0.0 collective-permute-start.1
  9.5 6.2 %collective-permute-done.c1 = bf16[64,2176]{1,0:T(8,128)(2,1)S(1)} collective-permute-done((bf16[64,2176]{1,0:T(8,128)(2,1)S(1)}, bf16[64,2176]{1,0:T(8,128)(2,1)S(1)}, u32[]{:S(2)}, u32[]{:S(2)}) %collective-permute-start) | collective-permute-done | bytes 278560 | tf_op jit(solution)/shard_map/ppermute | solution.py:52
  15.7 0.0 collective-permute-start.2
  15.8 3.2 %collective-permute-start.3 = (bf16[64,2176]{1,0:T(8,128)(2,1)S(1)}, bf16[64,2176]{1,0:T(8,128)(2,1)S(1)}, u32[]{:S(2)}, u32[]{:S(2)}) collective-permute-start(bf16[64,2176]{1,0:T(8,128)(2,1)S(1)} %prepare.1.c0), channel_id=1, source_target_pairs={{0,1},{1,0},{2,3},{3,2},{4,5},{5,4},{6,7},{7,6},{8,9},{9,8},{10,11... | collective-permute-start | bytes 835592 | tf_op jit(solution)/shard_map/ppermute | solution.py:52
  19.0 0.1 collective-permute-start.4
  19.1 0.4 collective-permute-start.5
  19.5 2.0 collective-permute-done.2.c3
  21.4 2.0 collective-permute-start.6
  23.5 0.1 pad_maximum_fusion
  23.6 1.0 fusion
  24.6 0.0 collective-permute-done.4.c5
  24.6 0.0 collective-permute-done.5.c6
  24.6 0.1 collective-permute-done.6.c7
  24.7 1.2 copy-done.3
  25.9 0.8 copy-done.6
  26.7 0.7 copy-done.9
  27.4 24.4 %attention.1 = (bf16[256,2048]{1,0:T(8,128)(2,1)S(1)}, bf16[256,2048]{1,0:T(8,128)(2,1)S(1)}) custom-call(bf16[64,2176]{1,0:T(8,128)(2,1)S(1)} %prepare.1.c0, bf16[64,2176]{1,0:T(8,128)(2,1)S(1)} %collective-permute-done.c1, bf16[64,2176]{1,0:T(8,128)(2,1)S(1)} %collective-permute-done.1.c2, bf16[64,2176]{1,0:T(8,128)(2,1)S(1)} %collective-permute-done.2.c3, ...), custom_call_target="tpu_custom_call" | custom-call | tf_op jit(solution)/shard_map/attention/pallas_call | solution.py:239
  51.8 0.0 copy-start.5
  51.9 0.0 copy-start.8
  51.9 0.0 copy-start.10
  51.9 0.6 collective-permute-start.7
  52.5 2.7 %collective-permute-start.14 = (bf16[352,2048]{1,0:T(8,128)(2,1)S(1)}, bf16[352,2048]{1,0:T(8,128)(2,1)S(1)}, u32[]{:S(2)}, u32[]{:S(2)}) collective-permute-start(bf16[352,2048]{1,0:T(8,128)(2,1)S(1)} %bitcast.22), channel_id=1, source_target_pairs={{0,32},{1,97},{2,34},{3,99},{4,36},{5,101},{6,38},{7,103},{8,40},{... | collective-permute-start | bytes 4325384 | tf_op jit(solution)/shard_map/ppermute | solution.py:48
  55.3 0.1 collective-permute-start.11
  55.4 0.0 collective-permute-done.10.refs_1_
  55.4 2.6 %collective-permute-start.12 = (bf16[2,352,2048]{2,1,0:T(8,128)(2,1)S(1)}, bf16[2,352,2048]{2,1,0:T(8,128)(2,1)S(1)}, u32[]{:S(2)}, u32[]{:S(2)}) collective-permute-start(bf16[2,352,2048]{2,1,0:T(8,128)(2,1)S(1)} %collective-permute-done.10.refs_1_), channel_id=1, source_target_pairs={{0,32},{1,97},{2,34},{3,99},{4,36},{5,101},{6,38},{7,103},{8,40},{... | collective-permute-start | bytes 8650760 | tf_op jit(solution)/shard_map/ppermute | solution.py:48
  58.0 0.1 add_convert_fusion.1
  58.1 3.0 %collective-permute-start.8 = (bf16[128,2048]{1,0:T(8,128)(2,1)S(1)}, bf16[128,2048]{1,0:T(8,128)(2,1)S(1)}, u32[]{:S(2)}, u32[]{:S(2)}) collective-permute-start(bf16[128,2048]{1,0:T(8,128)(2,1)S(1)} %add_convert_fusion.1), channel_id=1, source_target_pairs={{0,2},{1,7},{2,0},{3,5},{4,6},{5,3},{6,4},{7,1},{8,10},{9,15},{10,... | collective-permute-start | bytes 1572872 | tf_op jit(solution)/shard_map/ppermute | solution.py:52
  61.1 0.3 collective-permute-start.13
  61.4 10.2 %collective-permute-done.14.refs_6_ = bf16[352,2048]{1,0:T(8,128)(2,1)S(1)} collective-permute-done((bf16[352,2048]{1,0:T(8,128)(2,1)S(1)}, bf16[352,2048]{1,0:T(8,128)(2,1)S(1)}, u32[]{:S(2)}, u32[]{:S(2)}) %collective-permute-start.14) | collective-permute-done | bytes 1441824 | tf_op jit(solution)/shard_map/ppermute | solution.py:48
  71.7 0.3 collective-permute-start.15
  72.0 0.0 collective-permute-done.8.got_a
  72.0 0.1 add_convert_fusion.2
  72.1 0.8 collective-permute-start.9
  72.9 4.8 %collective-permute-done.9.got_b = bf16[64,2048]{1,0:T(8,128)(2,1)S(1)} collective-permute-done((bf16[64,2048]{1,0:T(8,128)(2,1)S(1)}, bf16[64,2048]{1,0:T(8,128)(2,1)S(1)}, u32[]{:S(2)}, u32[]{:S(2)}) %collective-permute-start.9) | collective-permute-done | bytes 262176 | tf_op jit(solution)/shard_map/ppermute | solution.py:52
  77.7 0.6 settle.1
  78.3 18.4 %all_to_all.10 = bf16[8,24,2048]{2,1,0:T(8,128)(2,1)S(1)} all-to-all(bf16[8,24,2048]{2,1,0:T(8,128)(2,1)S(1)} %bitcast.25), channel_id=1, replica_groups=mesh['req'=16,'head'=8] {'head'}, dimensions={0} | all-to-all | bytes 1572864 | tf_op jit(solution)/shard_map/all_to_all | solution.py:450
  96.7 2.5 %collective-permute-start.16 = (bf16[192,2048]{1,0:T(8,128)(2,1)S(1)}, bf16[192,2048]{1,0:T(8,128)(2,1)S(1)}, u32[]{:S(2)}, u32[]{:S(2)}) collective-permute-start(bf16[192,2048]{1,0:T(8,128)(2,1)S(1)} %bitcast.14), channel_id=1, source_target_pairs={{0,120},{1,41},{2,122},{3,43},{4,124},{5,45},{6,126},{7,47},{8,112... | collective-permute-start | bytes 2359304 | tf_op jit(solution)/shard_map/ppermute | solution.py:48
  99.3 0.0 collective-permute-done.13.refs_5_
  99.3 0.0 collective-permute-start.18
  99.3 0.0 collective-permute-done.15.refs_7_
  99.3 0.3 collective-permute-start.20
  99.6 3.0 %collective-permute-done.11.refs_2_ = bf16[2,352,2048]{2,1,0:T(8,128)(2,1)S(1)} collective-permute-done((bf16[2,352,2048]{2,1,0:T(8,128)(2,1)S(1)}, bf16[2,352,2048]{2,1,0:T(8,128)(2,1)S(1)}, u32[]{:S(2)}, u32[]{:S(2)}) %collective-permute-start.11) | collective-permute-done | bytes 2883616 | tf_op jit(solution)/shard_map/ppermute | solution.py:48
  102.6 47.8 %collective-permute-done.12.refs_3_ = bf16[2,352,2048]{2,1,0:T(8,128)(2,1)S(1)} collective-permute-done((bf16[2,352,2048]{2,1,0:T(8,128)(2,1)S(1)}, bf16[2,352,2048]{2,1,0:T(8,128)(2,1)S(1)}, u32[]{:S(2)}, u32[]{:S(2)}) %collective-permute-start.12) | collective-permute-done | bytes 2883616 | tf_op jit(solution)/shard_map/ppermute | solution.py:48
  150.3 3.2 %pack.1.weights = bf16[4224,2048]{1,0:T(8,128)(2,1)S(1)} custom-call(bf16[2,352,2048]{2,1,0:T(8,128)(2,1)S(1)} %bitcast.21, bf16[2,352,2048]{2,1,0:T(8,128)(2,1)S(1)} %collective-permute-done.10.refs_1_, bf16[2,352,2048]{2,1,0:T(8,128)(2,1)S(1)} %collective-permute-done.11.refs_2_, bf16[2,352,2048]{2,1,0:T(8,128)(2,1)S(1)} %collective-permute-done.12.refs_3_, ...), custom_call_target="tpu_custom_call" | custom-call | tf_op jit(solution)/shard_map/pack/pallas_call | solution.py:375
  153.5 5.2 %shard_map.137 = bf16[192,2048]{1,0:T(8,128)(2,1)S(1)} custom-call(bf16[192,2048]{1,0:T(8,128)(2,1)S(1)} %collective-permute-done.16.rows, bf16[4224,2048]{1,0:T(8,128)(2,1)S(1)} %pack.1.weights), custom_call_target="tpu_custom_call" | custom-call | tf_op jit(solution)/shard_map/pallas_call | solution.py:400
  158.7 0.1 collective-permute-start.17
  158.8 5.2 %shard_map.138 = bf16[192,2048]{1,0:T(8,128)(2,1)S(1)} custom-call(bf16[192,2048]{1,0:T(8,128)(2,1)S(1)} %collective-permute-done.18.rows, bf16[4224,2048]{1,0:T(8,128)(2,1)S(1)} %pack.1.weights), custom_call_target="tpu_custom_call" | custom-call | tf_op jit(solution)/shard_map/pallas_call | solution.py:400
  164.0 1.8 collective-permute-start.19
  165.7 5.1 %shard_map.139 = bf16[192,2048]{1,0:T(8,128)(2,1)S(1)} custom-call(bf16[192,2048]{1,0:T(8,128)(2,1)S(1)} %collective-permute-done.20.rows, bf16[4224,2048]{1,0:T(8,128)(2,1)S(1)} %pack.1.weights), custom_call_target="tpu_custom_call" | custom-call | tf_op jit(solution)/shard_map/pallas_call | solution.py:400
  170.9 1.2 collective-permute-start.21
  172.1 5.1 %shard_map.136 = bf16[192,2048]{1,0:T(8,128)(2,1)S(1)} custom-call(bf16[192,2048]{1,0:T(8,128)(2,1)S(1)} %bitcast.17, bf16[4224,2048]{1,0:T(8,128)(2,1)S(1)} %pack.1.weights), custom_call_target="tpu_custom_call" | custom-call | tf_op jit(solution)/shard_map/pallas_call | solution.py:400
  177.3 1.1 collective-permute-done.19
  178.4 3.7 %collective-permute-done.21 = bf16[192,2048]{1,0:T(8,128)(2,1)S(1)} collective-permute-done((bf16[192,2048]{1,0:T(8,128)(2,1)S(1)}, bf16[192,2048]{1,0:T(8,128)(2,1)S(1)}, u32[]{:S(2)}, u32[]{:S(2)}) %collective-permute-start.21) | collective-permute-done | bytes 786464 | tf_op jit(solution)/shard_map/ppermute | solution.py:48
  182.1 1.4 add_convert_fusion
  183.5 10.9 %all-to-all-start.1 = ((bf16[8,24,2048]{2,1,0:T(8,128)(2,1)}), bf16[8,24,2048]{2,1,0:T(8,128)(2,1)S(1)}, u32[]{:S(2)}, u32[]{:S(2)}) async-start(bf16[8,24,2048]{2,1,0:T(8,128)(2,1)} %bitcast.12), calls=%async_computation.1 | async-start | bytes 1572864 | tf_op jit(solution)/shard_map/all_to_all | solution.py:466
  194.4 0.4 weigh.1
  194.8 11.8 %all-to-all-done.1 = bf16[8,24,2048]{2,1,0:T(8,128)(2,1)S(1)} async-done(((bf16[8,24,2048]{2,1,0:T(8,128)(2,1)}), bf16[8,24,2048]{2,1,0:T(8,128)(2,1)S(1)}, u32[]{:S(2)}, u32[]{:S(2)}) %all-to-all-start.1) | async-done | bytes 786464 | tf_op jit(solution)/shard_map/all_to_all | solution.py:466
  206.6 1.1 finish.1
  (25 shorter events, 0.1 us)
Async XLA Ops:
  0.0 24.7 %copy-start.2 = (bf16[2048,256]{1,0:T(8,128)(2,1)S(1)}, bf16[2048,256]{1,0:T(8,128)(2,1)}, u32[]{:S(2)}) copy-start(bf16[2048,256]{1,0:T(8,128)(2,1)} %wk.1) | copy-start | bytes 3145732
  0.0 55.4 %collective-permute-start.10 = (bf16[2,352,2048]{2,1,0:T(8,128)(2,1)}, bf16[2,352,2048]{2,1,0:T(8,128)(2,1)S(1)}, u32[]{:S(2)}, u32[]{:S(2)}) collective-permute-start(bf16[2,352,2048]{2,1,0:T(8,128)(2,1)} %bitcast.19), channel_id=1, source_target_pairs={{0,8},{1,25},{2,10},{3,27},{4,12},{5,29},{6,14},{7,31},{8,0},{9,17... | collective-permute-start | bytes 8650760 | tf_op jit(solution)/shard_map/ppermute | solution.py:48
  3.3 0.9 copy-start.4
  4.2 0.7 copy-start.11
  4.9 0.7 copy-start.12
  5.7 10.1 %collective-permute-start = (bf16[64,2176]{1,0:T(8,128)(2,1)S(1)}, bf16[64,2176]{1,0:T(8,128)(2,1)S(1)}, u32[]{:S(2)}, u32[]{:S(2)}) collective-permute-start(bf16[64,2176]{1,0:T(8,128)(2,1)S(1)} %prepare.1.c0), channel_id=1, source_target_pairs={{0,2},{1,7},{2,0},{3,5},{4,6},{5,3},{6,4},{7,1},{8,10},{9,15},{10,... | collective-permute-start | bytes 835592 | tf_op jit(solution)/shard_map/ppermute | solution.py:52
  9.5 9.5 %collective-permute-start.1 = (bf16[64,2176]{1,0:T(8,128)(2,1)S(1)}, bf16[64,2176]{1,0:T(8,128)(2,1)S(1)}, u32[]{:S(2)}, u32[]{:S(2)}) collective-permute-start(bf16[64,2176]{1,0:T(8,128)(2,1)S(1)} %prepare.1.c0), channel_id=1, source_target_pairs={{0,6},{1,3},{2,4},{3,1},{4,2},{5,7},{6,0},{7,5},{8,14},{9,11},{10,... | collective-permute-start | bytes 835592 | tf_op jit(solution)/shard_map/ppermute | solution.py:52
  15.7 5.7 %collective-permute-start.2 = (bf16[64,2176]{1,0:T(8,128)(2,1)S(1)}, bf16[64,2176]{1,0:T(8,128)(2,1)S(1)}, u32[]{:S(2)}, u32[]{:S(2)}) collective-permute-start(bf16[64,2176]{1,0:T(8,128)(2,1)S(1)} %collective-permute-done.c1), channel_id=1, source_target_pairs={{0,6},{1,3},{2,4},{3,1},{4,2},{5,7},{6,0},{7,5},{8,14},{9,11},{10,... | collective-permute-start | bytes 835592 | tf_op jit(solution)/shard_map/ppermute | solution.py:52
  15.8 8.8 %collective-permute-start.3 = (bf16[64,2176]{1,0:T(8,128)(2,1)S(1)}, bf16[64,2176]{1,0:T(8,128)(2,1)S(1)}, u32[]{:S(2)}, u32[]{:S(2)}) collective-permute-start(bf16[64,2176]{1,0:T(8,128)(2,1)S(1)} %prepare.1.c0), channel_id=1, source_target_pairs={{0,1},{1,0},{2,3},{3,2},{4,5},{5,4},{6,7},{7,6},{8,9},{9,8},{10,11... | collective-permute-start | bytes 835592 | tf_op jit(solution)/shard_map/ppermute | solution.py:52
  19.0 5.6 %collective-permute-start.4 = (bf16[64,2176]{1,0:T(8,128)(2,1)S(1)}, bf16[64,2176]{1,0:T(8,128)(2,1)S(1)}, u32[]{:S(2)}, u32[]{:S(2)}) collective-permute-start(bf16[64,2176]{1,0:T(8,128)(2,1)S(1)} %collective-permute-done.c1), channel_id=1, source_target_pairs={{0,1},{1,0},{2,3},{3,2},{4,5},{5,4},{6,7},{7,6},{8,9},{9,8},{10,11... | collective-permute-start | bytes 835592 | tf_op jit(solution)/shard_map/ppermute | solution.py:52
  19.1 5.5 %collective-permute-start.5 = (bf16[64,2176]{1,0:T(8,128)(2,1)S(1)}, bf16[64,2176]{1,0:T(8,128)(2,1)S(1)}, u32[]{:S(2)}, u32[]{:S(2)}) collective-permute-start(bf16[64,2176]{1,0:T(8,128)(2,1)S(1)} %collective-permute-done.1.c2), channel_id=1, source_target_pairs={{0,1},{1,0},{2,3},{3,2},{4,5},{5,4},{6,7},{7,6},{8,9},{9,8},{10,11... | collective-permute-start | bytes 835592 | tf_op jit(solution)/shard_map/ppermute | solution.py:52
  21.4 3.2 %collective-permute-start.6 = (bf16[64,2176]{1,0:T(8,128)(2,1)S(1)}, bf16[64,2176]{1,0:T(8,128)(2,1)S(1)}, u32[]{:S(2)}, u32[]{:S(2)}) collective-permute-start(bf16[64,2176]{1,0:T(8,128)(2,1)S(1)} %collective-permute-done.2.c3), channel_id=1, source_target_pairs={{0,1},{1,0},{2,3},{3,2},{4,5},{5,4},{6,7},{7,6},{8,9},{9,8},{10,11... | collective-permute-start | bytes 835592 | tf_op jit(solution)/shard_map/ppermute | solution.py:52
  24.7 1.2 copy-start.3
  25.9 0.8 copy-start.6
  26.7 0.7 copy-start.9
  27.4 25.1 %copy-start.1 = (bf16[1,352,2048]{2,1,0:T(8,128)(2,1)S(1)}, bf16[1,352,2048]{2,1,0:T(8,128)(2,1)}, u32[]{:S(2)}) copy-start(bf16[1,352,2048]{2,1,0:T(8,128)(2,1)} %param.27) | copy-start | bytes 4325380
  27.4 27.8 %copy-start = (bf16[1,2048,2,352]{1,3,2,0:T(8,128)(2,1)S(1)}, bf16[1,2048,2,352]{1,3,2,0:T(8,128)(2,1)}, u32[]{:S(2)}) copy-start(bf16[1,2048,2,352]{1,3,2,0:T(8,128)(2,1)} %param.26) | copy-start | bytes 8650756
  51.8 25.8 %copy-start.5 = (bf16[64,2048]{1,0:T(8,128)(2,1)S(1)}, bf16[64,2048]{1,0:T(8,128)(2,1)}, u32[]{:S(2)}) copy-start(bf16[64,2048]{1,0:T(8,128)(2,1)} %hidden.3) | copy-start | bytes 786436
  51.9 25.8 %copy-start.8 = (f32[2048]{0:T(1024)S(1)}, f32[2048]{0:T(1024)}, u32[]{:S(2)}) copy-start(f32[2048]{0:T(1024)} %param.24) | copy-start | bytes 24580
  51.9 25.8 %copy-start.10 = (s32[64,2]{0,1:T(2,128)S(1)}, s32[64,2]{0,1:T(2,128)}, u32[]{:S(2)}) copy-start(s32[64,2]{0,1:T(2,128)} %param.17) | copy-start | bytes 1540
  51.9 6.1 %collective-permute-start.7 = (bf16[256,2048]{1,0:T(8,128)(2,1)S(1)}, bf16[256,2048]{1,0:T(8,128)(2,1)S(1)}, u32[]{:S(2)}, u32[]{:S(2)}) collective-permute-start(bf16[256,2048]{1,0:T(8,128)(2,1)S(1)} %get-tuple-element.12), channel_id=1, source_target_pairs={{0,1},{1,0},{2,3},{3,2},{4,5},{5,4},{6,7},{7,6},{8,9},{9,8},{10,11... | collective-permute-start | bytes 3145736 | tf_op jit(solution)/shard_map/ppermute | solution.py:52
  52.5 19.1 %collective-permute-start.14 = (bf16[352,2048]{1,0:T(8,128)(2,1)S(1)}, bf16[352,2048]{1,0:T(8,128)(2,1)S(1)}, u32[]{:S(2)}, u32[]{:S(2)}) collective-permute-start(bf16[352,2048]{1,0:T(8,128)(2,1)S(1)} %bitcast.22), channel_id=1, source_target_pairs={{0,32},{1,97},{2,34},{3,99},{4,36},{5,101},{6,38},{7,103},{8,40},{... | collective-permute-start | bytes 4325384 | tf_op jit(solution)/shard_map/ppermute | solution.py:48
  55.3 47.3 %collective-permute-start.11 = (bf16[2,352,2048]{2,1,0:T(8,128)(2,1)S(1)}, bf16[2,352,2048]{2,1,0:T(8,128)(2,1)S(1)}, u32[]{:S(2)}, u32[]{:S(2)}) collective-permute-start(bf16[2,352,2048]{2,1,0:T(8,128)(2,1)S(1)} %bitcast.20), channel_id=1, source_target_pairs={{0,32},{1,97},{2,34},{3,99},{4,36},{5,101},{6,38},{7,103},{8,40},{... | collective-permute-start | bytes 8650760 | tf_op jit(solution)/shard_map/ppermute | solution.py:48
  55.4 95.0 %collective-permute-start.12 = (bf16[2,352,2048]{2,1,0:T(8,128)(2,1)S(1)}, bf16[2,352,2048]{2,1,0:T(8,128)(2,1)S(1)}, u32[]{:S(2)}, u32[]{:S(2)}) collective-permute-start(bf16[2,352,2048]{2,1,0:T(8,128)(2,1)S(1)} %collective-permute-done.10.refs_1_), channel_id=1, source_target_pairs={{0,32},{1,97},{2,34},{3,99},{4,36},{5,101},{6,38},{7,103},{8,40},{... | collective-permute-start | bytes 8650760 | tf_op jit(solution)/shard_map/ppermute | solution.py:48
  58.1 13.9 %collective-permute-start.8 = (bf16[128,2048]{1,0:T(8,128)(2,1)S(1)}, bf16[128,2048]{1,0:T(8,128)(2,1)S(1)}, u32[]{:S(2)}, u32[]{:S(2)}) collective-permute-start(bf16[128,2048]{1,0:T(8,128)(2,1)S(1)} %add_convert_fusion.1), channel_id=1, source_target_pairs={{0,2},{1,7},{2,0},{3,5},{4,6},{5,3},{6,4},{7,1},{8,10},{9,15},{10,... | collective-permute-start | bytes 1572872 | tf_op jit(solution)/shard_map/ppermute | solution.py:52
  61.1 38.2 %collective-permute-start.13 = (bf16[352,2048]{1,0:T(8,128)(2,1)S(1)}, bf16[352,2048]{1,0:T(8,128)(2,1)S(1)}, u32[]{:S(2)}, u32[]{:S(2)}) collective-permute-start(bf16[352,2048]{1,0:T(8,128)(2,1)S(1)} %bitcast.23), channel_id=1, source_target_pairs={{0,8},{1,25},{2,10},{3,27},{4,12},{5,29},{6,14},{7,31},{8,0},{9,17... | collective-permute-start | bytes 4325384 | tf_op jit(solution)/shard_map/ppermute | solution.py:48
  71.7 27.6 %collective-permute-start.15 = (bf16[352,2048]{1,0:T(8,128)(2,1)S(1)}, bf16[352,2048]{1,0:T(8,128)(2,1)S(1)}, u32[]{:S(2)}, u32[]{:S(2)}) collective-permute-start(bf16[352,2048]{1,0:T(8,128)(2,1)S(1)} %collective-permute-done.14.refs_6_), channel_id=1, source_target_pairs={{0,8},{1,25},{2,10},{3,27},{4,12},{5,29},{6,14},{7,31},{8,0},{9,17... | collective-permute-start | bytes 4325384 | tf_op jit(solution)/shard_map/ppermute | solution.py:48
  72.1 5.6 %collective-permute-start.9 = (bf16[64,2048]{1,0:T(8,128)(2,1)S(1)}, bf16[64,2048]{1,0:T(8,128)(2,1)S(1)}, u32[]{:S(2)}, u32[]{:S(2)}) collective-permute-start(bf16[64,2048]{1,0:T(8,128)(2,1)S(1)} %add_convert_fusion.2), channel_id=1, source_target_pairs={{0,6},{1,3},{2,4},{3,1},{4,2},{5,7},{6,0},{7,5},{8,14},{9,11},{10,... | collective-permute-start | bytes 786440 | tf_op jit(solution)/shard_map/ppermute | solution.py:52
  96.7 56.8 %collective-permute-start.16 = (bf16[192,2048]{1,0:T(8,128)(2,1)S(1)}, bf16[192,2048]{1,0:T(8,128)(2,1)S(1)}, u32[]{:S(2)}, u32[]{:S(2)}) collective-permute-start(bf16[192,2048]{1,0:T(8,128)(2,1)S(1)} %bitcast.14), channel_id=1, source_target_pairs={{0,120},{1,41},{2,122},{3,43},{4,124},{5,45},{6,126},{7,47},{8,112... | collective-permute-start | bytes 2359304 | tf_op jit(solution)/shard_map/ppermute | solution.py:48
  99.3 59.5 %collective-permute-start.18 = (bf16[192,2048]{1,0:T(8,128)(2,1)S(1)}, bf16[192,2048]{1,0:T(8,128)(2,1)S(1)}, u32[]{:S(2)}, u32[]{:S(2)}) collective-permute-start(bf16[192,2048]{1,0:T(8,128)(2,1)S(1)} %bitcast.15), channel_id=1, source_target_pairs={{0,24},{1,9},{2,26},{3,11},{4,28},{5,13},{6,30},{7,15},{8,16},{9,1... | collective-permute-start | bytes 2359304 | tf_op jit(solution)/shard_map/ppermute | solution.py:48
  99.3 66.5 %collective-permute-start.20 = (bf16[192,2048]{1,0:T(8,128)(2,1)S(1)}, bf16[192,2048]{1,0:T(8,128)(2,1)S(1)}, u32[]{:S(2)}, u32[]{:S(2)}) collective-permute-start(bf16[192,2048]{1,0:T(8,128)(2,1)S(1)} %bitcast.16), channel_id=1, source_target_pairs={{0,96},{1,33},{2,98},{3,35},{4,100},{5,37},{6,102},{7,39},{8,104},... | collective-permute-start | bytes 2359304 | tf_op jit(solution)/shard_map/ppermute | solution.py:48
  158.7 18.6 %collective-permute-start.17 = (bf16[192,2048]{1,0:T(8,128)(2,1)S(1)}, bf16[192,2048]{1,0:T(8,128)(2,1)S(1)}, u32[]{:S(2)}, u32[]{:S(2)}) collective-permute-start(bf16[192,2048]{1,0:T(8,128)(2,1)S(1)} %shard_map.137), channel_id=1, source_target_pairs={{0,120},{1,41},{2,122},{3,43},{4,124},{5,45},{6,126},{7,47},{8,112... | collective-permute-start | bytes 2359304 | tf_op jit(solution)/shard_map/ppermute | solution.py:48
  164.0 14.4 %collective-permute-start.19 = (bf16[192,2048]{1,0:T(8,128)(2,1)S(1)}, bf16[192,2048]{1,0:T(8,128)(2,1)S(1)}, u32[]{:S(2)}, u32[]{:S(2)}) collective-permute-start(bf16[192,2048]{1,0:T(8,128)(2,1)S(1)} %shard_map.138), channel_id=1, source_target_pairs={{0,24},{1,9},{2,26},{3,11},{4,28},{5,13},{6,30},{7,15},{8,16},{9,1... | collective-permute-start | bytes 2359304 | tf_op jit(solution)/shard_map/ppermute | solution.py:48
  170.9 11.2 %collective-permute-start.21 = (bf16[192,2048]{1,0:T(8,128)(2,1)S(1)}, bf16[192,2048]{1,0:T(8,128)(2,1)S(1)}, u32[]{:S(2)}, u32[]{:S(2)}) collective-permute-start(bf16[192,2048]{1,0:T(8,128)(2,1)S(1)} %shard_map.139), channel_id=1, source_target_pairs={{0,96},{1,33},{2,98},{3,35},{4,100},{5,37},{6,102},{7,39},{8,104},... | collective-permute-start | bytes 2359304 | tf_op jit(solution)/shard_map/ppermute | solution.py:48
  183.5 10.9 %copy-start.7 = (f32[2048,8]{0,1:T(8,128)S(1)}, f32[2048,8]{0,1:T(8,128)}, u32[]{:S(2)}) copy-start(f32[2048,8]{0,1:T(8,128)} %param.25) | copy-start | bytes 196612
  183.5 23.1 %all-to-all-start.1 = ((bf16[8,24,2048]{2,1,0:T(8,128)(2,1)}), bf16[8,24,2048]{2,1,0:T(8,128)(2,1)S(1)}, u32[]{:S(2)}, u32[]{:S(2)}) async-start(bf16[8,24,2048]{2,1,0:T(8,128)(2,1)} %bitcast.12), calls=%async_computation.1 | async-start | bytes 1572864 | tf_op jit(solution)/shard_map/all_to_all | solution.py:466
where the time goes:
time: 208 us
  waiting for transfers between devices  90.7 us (44%)
  Pallas kernels  50.5 us (24%)
  starting transfers between devices  40.2 us (19%)
  blocking collectives  18.4 us (9%)
  local copies, waits for them, and re-layouts  5.08 us (2%)
  other arithmetic  2.69 us (1%)
    ppermute x12, waiting for transfers between devices, send_xy(): return lax.ppermute(v, AXES, pairs)  65.8 us
    pallas_call x1, Pallas kernels, attention(): pl.pallas_call(attention_body, grid_spec=spec, out_shape=[jax.ShapeDtypeS...  24.4 us
    pallas_call x4, Pallas kernels, experts(): pl.pallas_call(expert_body, in_specs=[vmem] * 2, out_specs=vmem, out_shap...  20.6 us
    all_to_all x1, blocking collectives, per_device(): lax.all_to_all(rows.reshape(8, SLOTS, D), 'head', split_axis=0, concat_ax...  18.4 us
    ppermute x12, starting transfers between devices, send_xy(): return lax.ppermute(v, AXES, pairs)  15.2 us
    ppermute x10, starting transfers between devices, send_h(): return lax.ppermute(v, 'head', pairs)  14.1 us
    ppermute x10, waiting for transfers between devices, send_h(): return lax.ppermute(v, 'head', pairs)  13.1 us
    all_to_all x1, waiting for transfers between devices, per_device(): lax.all_to_all(rows, 'head', split_axis=0, concat_axis=0, tiled=True)  11.8 us
  transfers between devices with their start and end apart: 23, of which 10 were waited for; matrix products, arithmetic and copies ran while one was open for 1% of the time, Pallas kernels for 24%

commit v1 on v0

--- a/solution.py
+++ b/solution.py
@@ -1,3 +1,5 @@
+import math
+
 import jax
 import jax.numpy as jnp
 from jax import lax
@@ -14,10 +16,12 @@
 SLOTS = 24
 HID = 352
 FF4 = 4 * HID
+CUT = 3 * HID // 2
 BF = jnp.bfloat16
 F32 = jnp.float32
 EPSILON = 1e-06
 ROPE_BASE = 10000.0
+SOFTMAX_SCALE = HD ** (-0.5) * math.log2(math.e)
 AXES = ("req", "head")
 
 
@@ -31,7 +35,7 @@
         r, h = divmod(i, 8)
         y, x = divmod(r, 4)
         parity = (h & 1) ^ flip
-        ny = mate(y, parity) if move_y else y
+        ny = mate(y, parity ^ 1) if move_y else y
         nx = mate(x, parity) if move_x else x
         pairs.append((i, (ny * 4 + nx) * 8 + h))
     return pairs
@@ -106,126 +110,139 @@
 
 def attention_body(
     c0, c1, c2, c3, c4, c5, c6, c7,
-    gain, router, cos_t, sin_t, wq, wk, wv, wo,
+    router, cos_t, sin_t, wq, wk, wv, wo,
     keep, send,
-    x_s, meta_s, q_s, k_s, v_s, rope_c, rope_s, gate_s, ctx_s, mix_s,
+    x_s, meta_s, named_s, q_s, k_s, v_s, rope_c, rope_s, gate_s, ctx_s, mix_s, wq_s, kv_w, wo_s, sems,
 ):
-    step = pl.program_id(0)
-
-    @pl.when(step == 0)
-    def _():
-        for place, ref in zip(head_order(False), (c0, c1, c2, c3, c4, c5, c6, c7)):
-            base = pl.multiple_of(place * ROWS, ROWS)
-            x_s[pl.ds(base, ROWS), :] = normalize(ref[:, :D], gain[...])
-            meta_s[pl.ds(base, ROWS), :] = ref[:, D:].astype(F32)
-        seg = meta_s[:, 0:1]
-        cos_all = cos_t[...]
-        sin_all = sin_t[...]
-        c_sel = jnp.broadcast_to(cos_t[0:1, :], (SEQ, HD))
-        s_sel = jnp.broadcast_to(sin_t[0:1, :], (SEQ, HD))
-        for number in (1, 2, 3):
-            start = jnp.sum(jnp.where(seg < float(number), 1.0, 0.0)).astype(jnp.int32)
-            start = jnp.minimum(start, SEQ - 1)
-            here = seg == float(number)
-            c_sel = jnp.where(here, cos_t[pl.ds(start, 1), :], c_sel)
-            s_sel = jnp.where(here, sin_t[pl.ds(start, 1), :], s_sel)
-        lane = lax.broadcasted_iota(jnp.int32, (SEQ, HD), 1)
-        rope_c[...] = cos_all * c_sel + sin_all * s_sel
-        turned = sin_all * c_sel - cos_all * s_sel
-        rope_s[...] = jnp.where(lane < HD // 2, -turned, turned)
-        x = x_s[...]
-        keys = matmul(x, wk[...])
-        for g in range(2):
-            one = keys[:, g * HD : (g + 1) * HD]
-            k_s[:, g * HD : (g + 1) * HD] = (
-                one * rope_c[...] + pltpu.roll(one, HD // 2, 1) * rope_s[...]
-            ).astype(BF)
-        v_s[...] = matmul(x, wv[...]).astype(BF)
-        logits3 = matmul_t(x, split_router(router[...]))
-        g0, g1 = picked_gates(logits3, meta_s[:, 1:2], meta_s[:, 2:3])
-        gate_s[:, 0:1] = g0
-        gate_s[:, 1:2] = g1
-
-    @pl.when(step < 8)
-    def _():
-        here = step.astype(F32)
-        query = matmul(x_s[...], wq[0])
+    query_copies = [
+        pltpu.make_async_copy(wq.at[e], wq_s.at[:, pl.ds(e * 256, 256)], sems.at[e]) for e in range(8)
+    ]
+    key_copy = pltpu.make_async_copy(wk, kv_w.at[:, pl.ds(0, 256)], sems.at[8])
+    value_copy = pltpu.make_async_copy(wv, kv_w.at[:, pl.ds(256, 256)], sems.at[9])
+    out_copy = pltpu.make_async_copy(wo, wo_s, sems.at[10])
+    key_copy.start()
+    value_copy.start()
+    for copy in query_copies:
+        copy.start()
+    out_copy.start()
+
+    for place, ref in zip(head_order(False), (c0, c1, c2, c3, c4, c5, c6, c7)):
+        base = pl.multiple_of(place * ROWS, ROWS)
+        x_s[pl.ds(base, ROWS), :] = ref[:, :D]
+        meta_s[pl.ds(base, ROWS), :] = ref[:, D:].astype(F32)
+    seg = meta_s[:, 0:1]
+    for j in range(2):
+        named_s[j] = jnp.broadcast_to(meta_s[:, 1 + j : 2 + j], (SEQ, HD))
+    cos_all = cos_t[...]
+    sin_all = sin_t[...]
+    c_sel = jnp.broadcast_to(cos_t[0:1, :], (SEQ, HD))
+    s_sel = jnp.broadcast_to(sin_t[0:1, :], (SEQ, HD))
+    for number in (1, 2, 3):
+        start = jnp.sum(jnp.where(seg < float(number), 1.0, 0.0)).astype(jnp.int32)
+        start = jnp.minimum(start, SEQ - 1)
+        here = seg == float(number)
+        c_sel = jnp.where(here, cos_t[pl.ds(start, 1), :], c_sel)
+        s_sel = jnp.where(here, sin_t[pl.ds(start, 1), :], s_sel)
+    lane = lax.broadcasted_iota(jnp.int32, (SEQ, HD), 1)
+    rope_c[...] = cos_all * c_sel + sin_all * s_sel
+    turned = sin_all * c_sel - cos_all * s_sel
+    rope_s[...] = jnp.where(lane < HD // 2, -turned, turned)
+    logits3 = matmul_t(x_s[...], split_router(router[...]))
+    g0, g1 = picked_gates(logits3, meta_s[:, 1:2], meta_s[:, 2:3])
+    gate_s[:, 0:1] = g0
+    gate_s[:, 1:2] = g1
+    key_copy.wait()
+    value_copy.wait()
+    both = matmul(x_s[...], kv_w[...])
+    v_s[...] = both[:, 256:].astype(BF)
+    for g in range(2):
+        one = both[:, g * HD : (g + 1) * HD]
+        k_s[:, g * HD : (g + 1) * HD] = (
+            one * rope_c[...] + pltpu.roll(one, HD // 2, 1) * rope_s[...]
+        ).astype(BF)
+    for copy in query_copies:
+        copy.wait()
+
+    def query_step(pair, carry):
+        here = (2 * pair).astype(F32)
+        query = matmul(x_s[...], wq_s[:, pl.ds(pl.multiple_of(pair * 512, 512), 512)])
         for j in range(2):
-            chosen = meta_s[:, 1 + j : 2 + j] == here
-            q_s[j] = jnp.where(chosen, query, q_s[j])
-
-    @pl.when(step == 7)
-    def _():
-        seg_row = jnp.transpose(meta_s[...])[0:1, :]
+            is_first = named_s[j] == here
+            is_second = named_s[j] == here + 1.0
+            for g in range(2):
+                cols = slice(g * HD, (g + 1) * HD)
+                other = query[:, 256 + g * HD : 256 + (g + 1) * HD]
+                q_s[j, :, cols] = jnp.where(
+                    is_first, query[:, cols], jnp.where(is_second, other, q_s[j, :, cols])
+                )
+        return carry
+
+    lax.fori_loop(0, 4, query_step, 0)
+    seg_row = jnp.transpose(meta_s[...])[0:1, :]
+    for block in range(4):
+        lo = max(0, block * 128 - 256)
+        hi = block * 128 + 128
+        rows = slice(block * 128, hi)
+        q_pos = lax.broadcasted_iota(jnp.int32, (128, hi - lo), 0) + block * 128
+        k_pos = lax.broadcasted_iota(jnp.int32, (128, hi - lo), 1) + lo
+        allowed = (meta_s[rows, 0:1] == seg_row[:, lo:hi]) & (k_pos <= q_pos)
         for g in range(2):
             cols = slice(g * HD, (g + 1) * HD)
-            for block in range(4):
-                lo = max(0, block * 128 - 256)
-                hi = block * 128 + 128
-                rows = slice(block * 128, hi)
-                parts = []
-                for j in range(2):
-                    one = q_s[j, rows, cols]
-                    parts.append(
-                        (one * rope_c[rows, :] + pltpu.roll(one, HD // 2, 1) * rope_s[rows, :]).astype(BF)
-                    )
-                query = jnp.concatenate(parts, axis=0)
-                scores = matmul_t(query, k_s[lo:hi, cols]) * HD ** (-0.5)
-                q_pos = lax.broadcasted_iota(jnp.int32, (128, hi - lo), 0) + block * 128
-                k_pos = lax.broadcasted_iota(jnp.int32, (128, hi - lo), 1) + lo
-                allowed = (meta_s[rows, 0:1] == seg_row[:, lo:hi]) & (k_pos <= q_pos)
-                allowed = jnp.concatenate([allowed.astype(F32)] * 2, axis=0) > 0.5
-                masked = jnp.where(allowed, scores, -1e30)
+            parts = []
+            for j in range(2):
+                one = q_s[j, rows, cols]
+                parts.append(
+                    (one * rope_c[rows, :] + pltpu.roll(one, HD // 2, 1) * rope_s[rows, :]).astype(BF)
+                )
+            scores = matmul_t(jnp.concatenate(parts, axis=0), k_s[lo:hi, cols])
+            powers, totals = [], []
+            for j in range(2):
+                masked = jnp.where(allowed, scores[j * 128 : (j + 1) * 128], -1e30)
                 largest = jnp.max(masked, axis=-1, keepdims=True)
-                exponent = jnp.exp(masked - largest)
-                total = jnp.sum(exponent, axis=-1, keepdims=True)
-                probs = (exponent / total).astype(BF)
-                context = matmul(probs, v_s[lo:hi, cols])
-                ctx_s[0, rows, cols] = context[:128]
-                ctx_s[1, rows, cols] = context[128:]
-        for i, place in enumerate(head_order(True)):
-            base = pl.multiple_of(place * ROWS, ROWS)
-            take = pl.ds(base, ROWS)
-            first = ctx_s[0, take, :].astype(BF).astype(F32) * gate_s[take, 0:1]
-            second = ctx_s[1, take, :].astype(BF).astype(F32) * gate_s[take, 1:2]
-            meta = meta_s[take, :]
-            for e in range(8):
-                mixed = jnp.where(meta[:, 1:2] == float(e), first, 0.0) + jnp.where(
-                    meta[:, 2:3] == float(e), second, 0.0
-                )
-                mix_s[i * ROWS : (i + 1) * ROWS, e * 256 : (e + 1) * 256] = mixed.astype(BF)
-
-    @pl.when(step >= 8)
-    def _():
-        weights = wo[...].reshape(8 * 256, 512)
-        out = matmul(mix_s[...], weights)
-        keep[...] = out[:256].astype(BF)
-        send[...] = out[256:].astype(BF)
-
-
-def attention(chunks, gain, router, cos_t, sin_t, w_query, w_key, w_value, w_out):
-    whole = lambda shape: pl.BlockSpec(shape, lambda i: (0,) * len(shape))
-    spec = pltpu.PrefetchScalarGridSpec(
-        num_scalar_prefetch=0,
-        grid=(12,),
-        in_specs=[whole((ROWS, D + META))] * 8
-        + [
-            whole((1, D)),
-            whole((8, D)),
-            whole((SEQ, HD)),
-            whole((SEQ, HD)),
-            pl.BlockSpec((1, D, 256), lambda i: (jnp.minimum(i, 7), 0, 0)),
-            whole((D, 256)),
-            whole((D, 256)),
-            pl.BlockSpec((8, 256, 512), lambda i: (0, 0, jnp.maximum(i - 8, 0))),
-        ],
-        out_specs=[
-            pl.BlockSpec((256, 512), lambda i: (0, jnp.maximum(i - 8, 0))),
-            pl.BlockSpec((256, 512), lambda i: (0, jnp.maximum(i - 8, 0))),
-        ],
+                exponent = jnp.exp2((masked - largest) * SOFTMAX_SCALE)
+                totals.append(jnp.sum(exponent, axis=-1, keepdims=True))
+                powers.append(exponent.astype(BF))
+            context = matmul(jnp.concatenate(powers, axis=0), v_s[lo:hi, cols])
+            for j in range(2):
+                weight = gate_s[rows, j : j + 1] / totals[j]
+                ctx_s[j, rows, cols] = context[j * 128 : (j + 1) * 128] * weight
+    for i, place in enumerate(head_order(True)):
+        base = pl.multiple_of(place * ROWS, ROWS)
+        take = pl.ds(base, ROWS)
+        first = ctx_s[0, take, :].astype(BF)
+        second = ctx_s[1, take, :].astype(BF)
+        one = jnp.broadcast_to(meta_s[take, 1:2], (ROWS, 256)).astype(BF)
+        two = jnp.broadcast_to(meta_s[take, 2:3], (ROWS, 256)).astype(BF)
+        zero = jnp.zeros((ROWS, 256), BF)
+        for e in range(8):
+            number = jnp.full((ROWS, 256), e, BF)
+            mix_s[i * ROWS : (i + 1) * ROWS, e * 256 : (e + 1) * 256] = jnp.where(
+                one == number, first, jnp.where(two == number, second, zero)
+            )
+
+    out_copy.wait()
+
+    def out_step(part, carry):
+        cols = pl.ds(pl.multiple_of(part * 512, 512), 512)
+        out = matmul(mix_s[...], wo_s[:, :, cols].reshape(8 * 256, 512))
+        keep[:, cols] = out[:256].astype(BF)
+        send[:, cols] = out[256:].astype(BF)
+        return carry
+
+    lax.fori_loop(0, 4, out_step, 0)
+
+
+def attention(chunks, router, cos_t, sin_t, w_query, w_key, w_value, w_out):
+    vmem = pl.BlockSpec(memory_space=pltpu.VMEM)
+    hbm = pl.BlockSpec(memory_space=pltpu.MemorySpace.HBM)
+    return pl.pallas_call(
+        attention_body,
+        in_specs=[vmem] * 11 + [hbm] * 4,
+        out_specs=[vmem, vmem],
         scratch_shapes=[
             pltpu.VMEM((SEQ, D), BF),
             pltpu.VMEM((SEQ, META), F32),
+            pltpu.VMEM((2, SEQ, HD), F32),
             pltpu.VMEM((2, SEQ, 256), F32),
             pltpu.VMEM((SEQ, 256), BF),
             pltpu.VMEM((SEQ, 256), BF),
@@ -234,37 +251,37 @@
             pltpu.VMEM((SEQ, META), F32),
             pltpu.VMEM((2, SEQ, 256), F32),
             pltpu.VMEM((SEQ, 8 * 256), BF),
+            pltpu.VMEM((D, 8 * 256), BF),
+            pltpu.VMEM((D, 512), BF),
+            pltpu.VMEM((8, 256, D), BF),
+            pltpu.SemaphoreType.DMA((11,)),
         ],
-    )
-    return pl.pallas_call(
-        attention_body,
-        grid_spec=spec,
         out_shape=[
             jax.ShapeDtypeStruct((256, D), BF),
             jax.ShapeDtypeStruct((256, D), BF),
         ],
         compiler_params=pltpu.CompilerParams(vmem_limit_bytes=40 << 20),
         name="attention",
-    )(*chunks, gain, router, cos_t, sin_t, w_query, w_key, w_value, w_out)
-
-
-def prepare_body(hidden, segments, routes, out):
-    out[:, :D] = hidden[...]
+    )(*chunks, router, cos_t, sin_t, w_query, w_key, w_value, w_out)
+
+
+def prepare_body(hidden, gain, segments, routes, out):
+    out[:, :D] = normalize(hidden[...], gain[...])
     rows = jnp.concatenate([segments[...], routes[...], jnp.zeros((5, ROWS), jnp.int32)], axis=0).astype(F32)
     rows = jnp.concatenate([rows, jnp.zeros((META - 8, ROWS), F32)], axis=0)
     out[:, D:] = jnp.transpose(rows).astype(BF)
 
 
-def prepare(hidden, segments, routes):
+def prepare(hidden, gain, segments, routes):
     vmem = pl.BlockSpec(memory_space=pltpu.VMEM)
     return pl.pallas_call(
         prepare_body,
-        in_specs=[vmem] * 3,
+        in_specs=[vmem] * 4,
         out_specs=vmem,
         out_shape=jax.ShapeDtypeStruct((ROWS, D + META), BF),
         compiler_params=pltpu.CompilerParams(vmem_limit_bytes=8 << 20),
         name="prepare",
-    )(hidden, segments, routes)
+    )(hidden, gain, segments, routes)
 
 
 def slot_rows(routes):
@@ -357,13 +374,21 @@
 
 
 def pack_body(*refs):
-    out, sems = refs[8], refs[9]
-    copies = []
+    gus, gu_d, gu_e, downs = refs[:3], refs[3], refs[4], refs[5:9]
+    out, sems = refs[9], refs[10]
+    pieces = []
+    for s in range(3):
+        pieces.append((gus[s].at[0], s * HID, HID))
+        pieces.append((gus[s].at[1], FF4 + s * HID, HID))
+    pieces.append((gu_d.at[pl.ds(0, HID), :], 3 * HID, HID))
+    pieces.append((gu_d.at[pl.ds(HID, CUT - HID), :], FF4 + 3 * HID, CUT - HID))
+    pieces.append((gu_e, FF4 + 2 * HID + CUT, 2 * HID - CUT))
     for s in range(4):
-        for part in range(3):
-            src = refs[s].at[part] if part < 2 else refs[4 + s]
-            place = pl.ds(part * FF4 + s * HID, HID)
-            copies.append(pltpu.make_async_copy(src, out.at[place, :], sems.at[part, s]))
+        pieces.append((downs[s], 2 * FF4 + s * HID, HID))
+    copies = [
+        pltpu.make_async_copy(src, out.at[pl.ds(place, size), :], sems.at[i])
+        for i, (src, place, size) in enumerate(pieces)
+    ]
     for copy in copies:
         copy.start()
     for copy in copies:
@@ -371,13 +396,12 @@
 
 
 def pack(gus, downs):
-    hbm = pl.BlockSpec(memory_space=pl.ANY)
     return pl.pallas_call(
         pack_body,
-        in_specs=[hbm] * 8,
+        in_specs=[pl.BlockSpec(memory_space=pltpu.MemorySpace.HBM)] * 9,
         out_specs=pl.BlockSpec(memory_space=pltpu.VMEM),
         out_shape=pltpu.VMEM((3 * FF4, D), BF),
-        scratch_shapes=[pltpu.SemaphoreType.DMA((3, 4))],
+        scratch_shapes=[pltpu.SemaphoreType.DMA((13,))],
         compiler_params=pltpu.CompilerParams(vmem_limit_bytes=4 << 20),
         name="pack",
     )(*gus, *downs)
@@ -405,6 +429,10 @@
         scratch_shapes=[pltpu.VMEM((rows.shape[0], FF4), BF)],
         compiler_params=pltpu.CompilerParams(vmem_limit_bytes=8 << 20),
     )(rows, weights)
+
+
+def in_hbm(array):
+    return pltpu.with_memory_space_constraint(array, pltpu.MemorySpace.HBM)
 
 
 def per_device(
@@ -425,13 +453,16 @@
 ):
     gu = jnp.transpose(w_gate_up[0], (1, 2, 0))
     down = w_down[0]
-    own = prepare(hidden_in, segment_ids, attn_routes.T)
+    own = prepare(in_hbm(hidden_in), in_hbm(attn_gain[None, :]), in_hbm(segment_ids), in_hbm(attn_routes.T))
     chunks = gather_head(own)
     gu_x = send_xy(gu, WX)
     down_y = send_xy(down, WY)
     gu_y = send_xy(gu, WY)
     down_x = send_xy(down, WX)
-    gu_d = send_xy(gu_x, WY)
+    gu_xr = gu_x.reshape(2 * HID, D)[:CUT]
+    gu_yr = gu_y.reshape(2 * HID, D)[CUT:]
+    gu_d = send_xy(gu_xr, WY)
+    gu_e = send_xy(gu_yr, WX)
     down_d = send_xy(down_y, WX)
 
     half = HD // 2
@@ -439,7 +470,8 @@
     angles = jnp.arange(SEQ, dtype=F32)[:, None] * jnp.concatenate([inverse, inverse])[None, :]
     cosine, sine = jnp.cos(angles), jnp.sin(angles)
     keep, send = attention(
-        chunks, attn_gain[None, :], attn_router.T, cosine, sine, w_query, w_key, w_value, w_out
+        chunks, in_hbm(attn_router.T), cosine, sine,
+        in_hbm(w_query), in_hbm(w_key), in_hbm(w_value), in_hbm(w_out),
     )
     got = send_h(send, HC)
     pass_a = (keep[128:].astype(F32) + got[128:].astype(F32)).astype(BF)
@@ -450,7 +482,7 @@
     arrived = lax.all_to_all(rows.reshape(8, SLOTS, D), "head", split_axis=0, concat_axis=0, tiled=True)
     high, low = weigh(residual, ffn_gain[None, :], ffn_router.T, ffn_routes.T)
     x_own = arrived.reshape(8 * SLOTS, D)
-    weights = pack((gu, gu_x, gu_y, gu_d), (down, down_x, down_y, down_d))
+    weights = pack((in_hbm(gu), in_hbm(gu_x), in_hbm(gu_y), gu_d, gu_e), (in_hbm(down), down_x, down_y, down_d))
     x_d = send_xy(x_own, TXY)
     x_x = send_xy(x_own, TX)
     x_y = send_xy(x_own, TY)

time: 208 us -> 202 us (0.971)
  waiting for transfers between devices: 90.7 us -> 84.2 us
  blocking collectives: 18.4 us -> 22.1 us
  starting transfers between devices: 40.2 us -> 43.8 us
  local copies, waits for them, and re-layouts: 5.08 us -> 1.64 us
  Pallas kernels: 50.5 us -> 47.1 us
    ppermute x12 -> x13, starting transfers between devices: 15.2 us -> 20.8 us  [send_xy(): return lax.ppermute(v, AXES, pairs)]
    all_to_all x1, starting transfers between devices: 10.9 us -> 6.53 us  [per_device(): lax.all_to_all(rows, 'head', split_axis=0, concat_axis=0, tiled=True)]
    unnamed x26 -> x16, local copies, waits for them, and re-layouts: 5.08 us -> 1.33 us
    all_to_all x1, blocking collectives: 18.4 us -> 22.1 us  [per_device(): lax.all_to_all(rows.reshape(8, SLOTS, D), 'head', split_axis=0, concat_ax...]
    ppermute x10, waiting for transfers between devices: 13.1 us -> 9.46 us  [send_h(): return lax.ppermute(v, 'head', pairs)]
    pallas_call x3, Pallas kernels: 27.7 us -> 24.3 us  [the longest x1 19 us: attention(): pl.pallas_call(attention_body, in_specs=[vmem] * 11 + [hbm] * 4, out_spec...]
    ppermute x12 -> x13, waiting for transfers between devices: 65.8 us -> 62.9 us  [send_xy(): return lax.ppermute(v, AXES, pairs)]
    ppermute x10, starting transfers between devices: 14.1 us -> 16.5 us  [send_h(): return lax.ppermute(v, 'head', pairs)]
  transfers between devices with their start and end apart: 23 -> 24, of which waited for: 10 -> 9; matrix products, arithmetic and copies ran while one was open for 1% -> 1% of each run, Pallas kernels for 24% -> 22%
where the time goes in v1:
time: 202 us
  waiting for transfers between devices  84.2 us (42%)
  Pallas kernels  47.1 us (23%)
  starting transfers between devices  43.8 us (22%)
  blocking collectives  22.1 us (11%)
  other arithmetic  2.7 us (1%)
    ppermute x13, waiting for transfers between devices, send_xy(): return lax.ppermute(v, AXES, pairs)  62.9 us
    all_to_all x1, blocking collectives, per_device(): lax.all_to_all(rows.reshape(8, SLOTS, D), 'head', split_axis=0, concat_ax...  22.1 us
    ppermute x13, starting transfers between devices, send_xy(): return lax.ppermute(v, AXES, pairs)  20.8 us
    pallas_call x4, Pallas kernels, experts(): pl.pallas_call(expert_body, in_specs=[vmem] * 2, out_specs=vmem, out_shap...  20.6 us
    pallas_call x1, Pallas kernels, attention(): pl.pallas_call(attention_body, in_specs=[vmem] * 11 + [hbm] * 4, out_spec...  19 us
    ppermute x10, starting transfers between devices, send_h(): return lax.ppermute(v, 'head', pairs)  16.5 us
    all_to_all x1, waiting for transfers between devices, per_device(): lax.all_to_all(rows, 'head', split_axis=0, concat_axis=0, tiled=True)  11.8 us
    ppermute x10, waiting for transfers between devices, send_h(): return lax.ppermute(v, 'head', pairs)  9.46 us
  transfers between devices with their start and end apart: 24, of which 9 were waited for; matrix products, arithmetic and copies ran while one was open for 1% of the time, Pallas kernels for 22%

profile of v1, /device:TPU:1, one launch (start us, length us, event | category | flops | bytes accessed | tf_op | source)
XLA Modules:
  0.0 201.7 jit_solution(2309579289399000335)
XLA Ops:
  0.0 1.1 prepare.1.c0
  1.1 4.7 %collective-permute-start = (bf16[64,2176]{1,0:T(8,128)(2,1)S(1)}, bf16[64,2176]{1,0:T(8,128)(2,1)S(1)}, u32[]{:S(2)}, u32[]{:S(2)}) collective-permute-start(bf16[64,2176]{1,0:T(8,128)(2,1)S(1)} %prepare.1.c0), channel_id=1, source_target_pairs={{0,2},{1,7},{2,0},{3,5},{4,6},{5,3},{6,4},{7,1},{8,10},{9,15},{10,... | collective-permute-start | bytes 835592 | tf_op jit(solution)/shard_map/ppermute | solution.py:56
  5.8 2.5 %collective-permute-start.10 = (bf16[2,352,2048]{2,1,0:T(8,128)(2,1)}, bf16[2,352,2048]{2,1,0:T(8,128)(2,1)S(1)}, u32[]{:S(2)}, u32[]{:S(2)}) collective-permute-start(bf16[2,352,2048]{2,1,0:T(8,128)(2,1)} %bitcast.29), channel_id=1, source_target_pairs={{0,8},{1,25},{2,10},{3,27},{4,12},{5,29},{6,14},{7,31},{8,0},{9,17... | collective-permute-start | bytes 8650760 | tf_op jit(solution)/shard_map/ppermute | solution.py:52
  8.3 0.0 collective-permute-start.1
  8.3 1.5 collective-permute-done.c1
  9.7 0.0 collective-permute-start.2
  9.7 5.1 %collective-permute-start.3 = (bf16[64,2176]{1,0:T(8,128)(2,1)S(1)}, bf16[64,2176]{1,0:T(8,128)(2,1)S(1)}, u32[]{:S(2)}, u32[]{:S(2)}) collective-permute-start(bf16[64,2176]{1,0:T(8,128)(2,1)S(1)} %prepare.1.c0), channel_id=1, source_target_pairs={{0,1},{1,0},{2,3},{3,2},{4,5},{5,4},{6,7},{7,6},{8,9},{9,8},{10,11... | collective-permute-start | bytes 835592 | tf_op jit(solution)/shard_map/ppermute | solution.py:56
  14.9 0.1 collective-permute-start.4
  14.9 0.0 collective-permute-done.1.c2
  14.9 0.4 collective-permute-start.5
  15.4 1.6 collective-permute-done.2.c3
  16.9 2.4 %collective-permute-start.6 = (bf16[64,2176]{1,0:T(8,128)(2,1)S(1)}, bf16[64,2176]{1,0:T(8,128)(2,1)S(1)}, u32[]{:S(2)}, u32[]{:S(2)}) collective-permute-start(bf16[64,2176]{1,0:T(8,128)(2,1)S(1)} %collective-permute-done.2.c3), channel_id=1, source_target_pairs={{0,1},{1,0},{2,3},{3,2},{4,5},{5,4},{6,7},{7,6},{8,9},{9,8},{10,11... | collective-permute-start | bytes 835592 | tf_op jit(solution)/shard_map/ppermute | solution.py:56
  19.4 0.1 pad_maximum_fusion
  19.4 1.0 fusion
  20.4 0.0 collective-permute-done.3.c4
  20.4 0.0 collective-permute-done.4.c5
  20.4 0.0 collective-permute-done.5.c6
  20.5 0.1 collective-permute-done.6.c7
  20.6 19.0 %attention.1 = (bf16[256,2048]{1,0:T(8,128)(2,1)S(1)}, bf16[256,2048]{1,0:T(8,128)(2,1)S(1)}) custom-call(bf16[64,2176]{1,0:T(8,128)(2,1)S(1)} %prepare.1.c0, bf16[64,2176]{1,0:T(8,128)(2,1)S(1)} %collective-permute-done.c1, bf16[64,2176]{1,0:T(8,128)(2,1)S(1)} %collective-permute-done.1.c2, bf16[64,2176]{1,0:T(8,128)(2,1)S(1)} %collective-permute-done.2.c3, ...), custom_call_target="tpu_custom_call" | custom-call | tf_op jit(solution)/shard_map/attention/pallas_call | solution.py:238
  39.5 0.5 collective-permute-start.7
  40.0 1.3 collective-permute-start.11
  41.3 0.2 collective-permute-start.15
  41.5 0.8 collective-permute-done.7.got
  42.3 0.1 add_convert_fusion.1
  42.4 3.0 %collective-permute-start.8 = (bf16[128,2048]{1,0:T(8,128)(2,1)S(1)}, bf16[128,2048]{1,0:T(8,128)(2,1)S(1)}, u32[]{:S(2)}, u32[]{:S(2)}) collective-permute-start(bf16[128,2048]{1,0:T(8,128)(2,1)S(1)} %add_convert_fusion.1), channel_id=1, source_target_pairs={{0,2},{1,7},{2,0},{3,5},{4,6},{5,3},{6,4},{7,1},{8,10},{9,15},{10,... | collective-permute-start | bytes 1572872 | tf_op jit(solution)/shard_map/ppermute | solution.py:56
  45.5 3.1 %collective-permute-start.14 = (bf16[352,2048]{1,0:T(8,128)(2,1)S(1)}, bf16[352,2048]{1,0:T(8,128)(2,1)S(1)}, u32[]{:S(2)}, u32[]{:S(2)}) collective-permute-start(bf16[352,2048]{1,0:T(8,128)(2,1)S(1)} %bitcast.34), channel_id=1, source_target_pairs={{0,8},{1,25},{2,10},{3,27},{4,12},{5,29},{6,14},{7,31},{8,0},{9,17... | collective-permute-start | bytes 4325384 | tf_op jit(solution)/shard_map/ppermute | solution.py:52
  48.5 40.5 %collective-permute-done.15.refs_7_ = bf16[352,2048]{1,0:T(8,128)(2,1)S(1)} collective-permute-done((bf16[352,2048]{1,0:T(8,128)(2,1)S(1)}, bf16[352,2048]{1,0:T(8,128)(2,1)S(1)}, u32[]{:S(2)}, u32[]{:S(2)}) %collective-permute-start.15) | collective-permute-done | bytes 1441824 | tf_op jit(solution)/shard_map/ppermute | solution.py:52
  89.1 3.1 %collective-permute-start.16 = (bf16[352,2048]{1,0:T(8,128)(2,1)S(1)}, bf16[352,2048]{1,0:T(8,128)(2,1)S(1)}, u32[]{:S(2)}, u32[]{:S(2)}) collective-permute-start(bf16[352,2048]{1,0:T(8,128)(2,1)S(1)} %collective-permute-done.15.refs_7_), channel_id=1, source_target_pairs={{0,8},{1,25},{2,10},{3,27},{4,12},{5,29},{6,14},{7,31},{8,0},{9,17... | collective-permute-start | bytes 4325384 | tf_op jit(solution)/shard_map/ppermute | solution.py:52
  92.1 0.0 collective-permute-done.10.refs_1_
  92.2 0.0 copy-start.3
  92.2 0.2 slice.31
  92.4 1.3 copy-done.4
  93.7 1.3 collective-permute-start.12
  95.0 0.0 collective-permute-done.8.got_a
  95.0 0.1 add_convert_fusion.2
  95.1 0.3 collective-permute-start.9
  95.4 5.5 %collective-permute-done.9.got_b = bf16[64,2048]{1,0:T(8,128)(2,1)S(1)} collective-permute-done((bf16[64,2048]{1,0:T(8,128)(2,1)S(1)}, bf16[64,2048]{1,0:T(8,128)(2,1)S(1)}, u32[]{:S(2)}, u32[]{:S(2)}) %collective-permute-start.9) | collective-permute-done | bytes 262176 | tf_op jit(solution)/shard_map/ppermute | solution.py:56
  100.9 0.6 settle.1
  101.5 22.1 %all_to_all.10 = bf16[8,24,2048]{2,1,0:T(8,128)(2,1)S(1)} all-to-all(bf16[8,24,2048]{2,1,0:T(8,128)(2,1)S(1)} %bitcast.21), channel_id=1, replica_groups=mesh['req'=16,'head'=8] {'head'}, dimensions={0} | all-to-all | bytes 1572864 | tf_op jit(solution)/shard_map/all_to_all | solution.py:482
  123.6 0.0 collective-permute-start.17
  123.6 1.1 collective-permute-start.19
  124.8 0.0 collective-permute-done.11.refs_2_
  124.8 2.7 %collective-permute-start.21 = (bf16[192,2048]{1,0:T(8,128)(2,1)S(1)}, bf16[192,2048]{1,0:T(8,128)(2,1)S(1)}, u32[]{:S(2)}, u32[]{:S(2)}) collective-permute-start(bf16[192,2048]{1,0:T(8,128)(2,1)S(1)} %bitcast.18), channel_id=1, source_target_pairs={{0,32},{1,97},{2,34},{3,99},{4,36},{5,101},{6,38},{7,103},{8,40},{... | collective-permute-start | bytes 2359304 | tf_op jit(solution)/shard_map/ppermute | solution.py:52
  127.5 0.1 slice.32
  127.6 0.0 collective-permute-done.16.refs_8_
  127.6 1.3 collective-permute-start.13
  128.9 18.2 %collective-permute-done.13.refs_4_ = bf16[176,2048]{1,0:T(8,128)(2,1)S(1)} collective-permute-done((bf16[176,2048]{1,0:T(8,128)(2,1)S(1)}, bf16[176,2048]{1,0:T(8,128)(2,1)S(1)}, u32[]{:S(2)}, u32[]{:S(2)}) %collective-permute-start.13) | collective-permute-done | bytes 720928 | tf_op jit(solution)/shard_map/ppermute | solution.py:52
  147.0 4.2 %pack.1.weights = bf16[4224,2048]{1,0:T(8,128)(2,1)S(1)} custom-call(bf16[2,352,2048]{2,1,0:T(8,128)(2,1)} %bitcast.30, bf16[2,352,2048]{2,1,0:T(8,128)(2,1)} %copy-done.4, bf16[2,352,2048]{2,1,0:T(8,128)(2,1)} %copy-done.5, bf16[528,2048]{1,0:T(8,128)(2,1)S(1)} %collective-permute-done.12.refs_3_, bf16[176,2048]{1,0:T(8,128)(2,1)S(1)} %collective-permute-done.13.refs_4_, ...), custom_call_target="tpu_custom_call" | custom-call | tf_op jit(solution)/shard_map/pack/pallas_call | solution.py:399
  151.3 0.0 collective-permute-done.17.rows
  151.3 5.2 %shard_map.137 = bf16[192,2048]{1,0:T(8,128)(2,1)S(1)} custom-call(bf16[192,2048]{1,0:T(8,128)(2,1)S(1)} %collective-permute-done.17.rows, bf16[4224,2048]{1,0:T(8,128)(2,1)S(1)} %pack.1.weights), custom_call_target="tpu_custom_call" | custom-call | tf_op jit(solution)/shard_map/pallas_call | solution.py:424
  156.4 0.1 collective-permute-start.18
  156.5 0.0 collective-permute-done.19.rows
  156.6 5.2 %shard_map.138 = bf16[192,2048]{1,0:T(8,128)(2,1)S(1)} custom-call(bf16[192,2048]{1,0:T(8,128)(2,1)S(1)} %collective-permute-done.19.rows, bf16[4224,2048]{1,0:T(8,128)(2,1)S(1)} %pack.1.weights), custom_call_target="tpu_custom_call" | custom-call | tf_op jit(solution)/shard_map/pallas_call | solution.py:424
  161.7 1.5 collective-permute-start.20
  163.2 5.1 %shard_map.139 = bf16[192,2048]{1,0:T(8,128)(2,1)S(1)} custom-call(bf16[192,2048]{1,0:T(8,128)(2,1)S(1)} %collective-permute-done.21.rows, bf16[4224,2048]{1,0:T(8,128)(2,1)S(1)} %pack.1.weights), custom_call_target="tpu_custom_call" | custom-call | tf_op jit(solution)/shard_map/pallas_call | solution.py:424
  168.3 2.8 %collective-permute-start.22 = (bf16[192,2048]{1,0:T(8,128)(2,1)S(1)}, bf16[192,2048]{1,0:T(8,128)(2,1)S(1)}, u32[]{:S(2)}, u32[]{:S(2)}) collective-permute-start(bf16[192,2048]{1,0:T(8,128)(2,1)S(1)} %shard_map.139), channel_id=1, source_target_pairs={{0,32},{1,97},{2,34},{3,99},{4,36},{5,101},{6,38},{7,103},{8,40},{... | collective-permute-start | bytes 2359304 | tf_op jit(solution)/shard_map/ppermute | solution.py:52
  171.1 5.2 %shard_map.136 = bf16[192,2048]{1,0:T(8,128)(2,1)S(1)} custom-call(bf16[192,2048]{1,0:T(8,128)(2,1)S(1)} %bitcast.19, bf16[4224,2048]{1,0:T(8,128)(2,1)S(1)} %pack.1.weights), custom_call_target="tpu_custom_call" | custom-call | tf_op jit(solution)/shard_map/pallas_call | solution.py:424
  176.3 0.0 collective-permute-done.20
  176.3 4.2 %collective-permute-done.22 = bf16[192,2048]{1,0:T(8,128)(2,1)S(1)} collective-permute-done((bf16[192,2048]{1,0:T(8,128)(2,1)S(1)}, bf16[192,2048]{1,0:T(8,128)(2,1)S(1)}, u32[]{:S(2)}, u32[]{:S(2)}) %collective-permute-start.22) | collective-permute-done | bytes 786464 | tf_op jit(solution)/shard_map/ppermute | solution.py:52
  180.5 1.4 add_convert_fusion
  181.9 6.5 %all-to-all-start.1 = ((bf16[8,24,2048]{2,1,0:T(8,128)(2,1)}), bf16[8,24,2048]{2,1,0:T(8,128)(2,1)S(1)}, u32[]{:S(2)}, u32[]{:S(2)}) async-start(bf16[8,24,2048]{2,1,0:T(8,128)(2,1)} %bitcast.14), calls=%async_computation.1 | async-start | bytes 1572864 | tf_op jit(solution)/shard_map/all_to_all | solution.py:498
  188.4 0.4 weigh.1
  188.8 11.8 %all-to-all-done.1 = bf16[8,24,2048]{2,1,0:T(8,128)(2,1)S(1)} async-done(((bf16[8,24,2048]{2,1,0:T(8,128)(2,1)}), bf16[8,24,2048]{2,1,0:T(8,128)(2,1)S(1)}, u32[]{:S(2)}, u32[]{:S(2)}) %all-to-all-start.1) | async-done | bytes 786464 | tf_op jit(solution)/shard_map/all_to_all | solution.py:498
  200.6 1.1 finish.1
  (19 shorter events, 0.0 us)
Async XLA Ops:
  1.1 8.6 %collective-permute-start = (bf16[64,2176]{1,0:T(8,128)(2,1)S(1)}, bf16[64,2176]{1,0:T(8,128)(2,1)S(1)}, u32[]{:S(2)}, u32[]{:S(2)}) collective-permute-start(bf16[64,2176]{1,0:T(8,128)(2,1)S(1)} %prepare.1.c0), channel_id=1, source_target_pairs={{0,2},{1,7},{2,0},{3,5},{4,6},{5,3},{6,4},{7,1},{8,10},{9,15},{10,... | collective-permute-start | bytes 835592 | tf_op jit(solution)/shard_map/ppermute | solution.py:56
  5.8 86.3 %collective-permute-start.10 = (bf16[2,352,2048]{2,1,0:T(8,128)(2,1)}, bf16[2,352,2048]{2,1,0:T(8,128)(2,1)S(1)}, u32[]{:S(2)}, u32[]{:S(2)}) collective-permute-start(bf16[2,352,2048]{2,1,0:T(8,128)(2,1)} %bitcast.29), channel_id=1, source_target_pairs={{0,8},{1,25},{2,10},{3,27},{4,12},{5,29},{6,14},{7,31},{8,0},{9,17... | collective-permute-start | bytes 8650760 | tf_op jit(solution)/shard_map/ppermute | solution.py:52
  8.3 6.7 %collective-permute-start.1 = (bf16[64,2176]{1,0:T(8,128)(2,1)S(1)}, bf16[64,2176]{1,0:T(8,128)(2,1)S(1)}, u32[]{:S(2)}, u32[]{:S(2)}) collective-permute-start(bf16[64,2176]{1,0:T(8,128)(2,1)S(1)} %prepare.1.c0), channel_id=1, source_target_pairs={{0,6},{1,3},{2,4},{3,1},{4,2},{5,7},{6,0},{7,5},{8,14},{9,11},{10,... | collective-permute-start | bytes 835592 | tf_op jit(solution)/shard_map/ppermute | solution.py:56
  9.7 7.2 %collective-permute-start.2 = (bf16[64,2176]{1,0:T(8,128)(2,1)S(1)}, bf16[64,2176]{1,0:T(8,128)(2,1)S(1)}, u32[]{:S(2)}, u32[]{:S(2)}) collective-permute-start(bf16[64,2176]{1,0:T(8,128)(2,1)S(1)} %collective-permute-done.c1), channel_id=1, source_target_pairs={{0,6},{1,3},{2,4},{3,1},{4,2},{5,7},{6,0},{7,5},{8,14},{9,11},{10,... | collective-permute-start | bytes 835592 | tf_op jit(solution)/shard_map/ppermute | solution.py:56
  9.7 10.7 %collective-permute-start.3 = (bf16[64,2176]{1,0:T(8,128)(2,1)S(1)}, bf16[64,2176]{1,0:T(8,128)(2,1)S(1)}, u32[]{:S(2)}, u32[]{:S(2)}) collective-permute-start(bf16[64,2176]{1,0:T(8,128)(2,1)S(1)} %prepare.1.c0), channel_id=1, source_target_pairs={{0,1},{1,0},{2,3},{3,2},{4,5},{5,4},{6,7},{7,6},{8,9},{9,8},{10,11... | collective-permute-start | bytes 835592 | tf_op jit(solution)/shard_map/ppermute | solution.py:56
  14.9 5.6 %collective-permute-start.4 = (bf16[64,2176]{1,0:T(8,128)(2,1)S(1)}, bf16[64,2176]{1,0:T(8,128)(2,1)S(1)}, u32[]{:S(2)}, u32[]{:S(2)}) collective-permute-start(bf16[64,2176]{1,0:T(8,128)(2,1)S(1)} %collective-permute-done.c1), channel_id=1, source_target_pairs={{0,1},{1,0},{2,3},{3,2},{4,5},{5,4},{6,7},{7,6},{8,9},{9,8},{10,11... | collective-permute-start | bytes 835592 | tf_op jit(solution)/shard_map/ppermute | solution.py:56
  14.9 5.5 %collective-permute-start.5 = (bf16[64,2176]{1,0:T(8,128)(2,1)S(1)}, bf16[64,2176]{1,0:T(8,128)(2,1)S(1)}, u32[]{:S(2)}, u32[]{:S(2)}) collective-permute-start(bf16[64,2176]{1,0:T(8,128)(2,1)S(1)} %collective-permute-done.1.c2), channel_id=1, source_target_pairs={{0,1},{1,0},{2,3},{3,2},{4,5},{5,4},{6,7},{7,6},{8,9},{9,8},{10,11... | collective-permute-start | bytes 835592 | tf_op jit(solution)/shard_map/ppermute | solution.py:56
  16.9 3.6 %collective-permute-start.6 = (bf16[64,2176]{1,0:T(8,128)(2,1)S(1)}, bf16[64,2176]{1,0:T(8,128)(2,1)S(1)}, u32[]{:S(2)}, u32[]{:S(2)}) collective-permute-start(bf16[64,2176]{1,0:T(8,128)(2,1)S(1)} %collective-permute-done.2.c3), channel_id=1, source_target_pairs={{0,1},{1,0},{2,3},{3,2},{4,5},{5,4},{6,7},{7,6},{8,9},{9,8},{10,11... | collective-permute-start | bytes 835592 | tf_op jit(solution)/shard_map/ppermute | solution.py:56
  20.6 19.4 %copy-start.6 = (bf16[1,2048,2,352]{1,3,2,0:T(8,128)(2,1)S(1)}, bf16[1,2048,2,352]{1,3,2,0:T(8,128)(2,1)}, u32[]{:S(2)}) copy-start(bf16[1,2048,2,352]{1,3,2,0:T(8,128)(2,1)} %param.26) | copy-start | bytes 8650756
  20.6 20.7 %copy-start.7 = (bf16[1,352,2048]{2,1,0:T(8,128)(2,1)S(1)}, bf16[1,352,2048]{2,1,0:T(8,128)(2,1)}, u32[]{:S(2)}) copy-start(bf16[1,352,2048]{2,1,0:T(8,128)(2,1)} %param.27) | copy-start | bytes 4325380
  39.5 2.7 %collective-permute-start.7 = (bf16[256,2048]{1,0:T(8,128)(2,1)S(1)}, bf16[256,2048]{1,0:T(8,128)(2,1)S(1)}, u32[]{:S(2)}, u32[]{:S(2)}) collective-permute-start(bf16[256,2048]{1,0:T(8,128)(2,1)S(1)} %get-tuple-element.12), channel_id=1, source_target_pairs={{0,1},{1,0},{2,3},{3,2},{4,5},{5,4},{6,7},{7,6},{8,9},{9,8},{10,11... | collective-permute-start | bytes 3145736 | tf_op jit(solution)/shard_map/ppermute | solution.py:56
  40.0 84.8 %collective-permute-start.11 = (bf16[2,352,2048]{2,1,0:T(8,128)(2,1)S(1)}, bf16[2,352,2048]{2,1,0:T(8,128)(2,1)S(1)}, u32[]{:S(2)}, u32[]{:S(2)}) collective-permute-start(bf16[2,352,2048]{2,1,0:T(8,128)(2,1)S(1)} %bitcast.31), channel_id=1, source_target_pairs={{0,96},{1,33},{2,98},{3,35},{4,100},{5,37},{6,102},{7,39},{8,104},... | collective-permute-start | bytes 8650760 | tf_op jit(solution)/shard_map/ppermute | solution.py:52
  41.3 47.8 %collective-permute-start.15 = (bf16[352,2048]{1,0:T(8,128)(2,1)S(1)}, bf16[352,2048]{1,0:T(8,128)(2,1)S(1)}, u32[]{:S(2)}, u32[]{:S(2)}) collective-permute-start(bf16[352,2048]{1,0:T(8,128)(2,1)S(1)} %bitcast.33), channel_id=1, source_target_pairs={{0,96},{1,33},{2,98},{3,35},{4,100},{5,37},{6,102},{7,39},{8,104},... | collective-permute-start | bytes 4325384 | tf_op jit(solution)/shard_map/ppermute | solution.py:52
  42.4 52.6 %collective-permute-start.8 = (bf16[128,2048]{1,0:T(8,128)(2,1)S(1)}, bf16[128,2048]{1,0:T(8,128)(2,1)S(1)}, u32[]{:S(2)}, u32[]{:S(2)}) collective-permute-start(bf16[128,2048]{1,0:T(8,128)(2,1)S(1)} %add_convert_fusion.1), channel_id=1, source_target_pairs={{0,2},{1,7},{2,0},{3,5},{4,6},{5,3},{6,4},{7,1},{8,10},{9,15},{10,... | collective-permute-start | bytes 1572872 | tf_op jit(solution)/shard_map/ppermute | solution.py:56
  45.5 78.2 %collective-permute-start.14 = (bf16[352,2048]{1,0:T(8,128)(2,1)S(1)}, bf16[352,2048]{1,0:T(8,128)(2,1)S(1)}, u32[]{:S(2)}, u32[]{:S(2)}) collective-permute-start(bf16[352,2048]{1,0:T(8,128)(2,1)S(1)} %bitcast.34), channel_id=1, source_target_pairs={{0,8},{1,25},{2,10},{3,27},{4,12},{5,29},{6,14},{7,31},{8,0},{9,17... | collective-permute-start | bytes 4325384 | tf_op jit(solution)/shard_map/ppermute | solution.py:52
  89.1 38.5 %collective-permute-start.16 = (bf16[352,2048]{1,0:T(8,128)(2,1)S(1)}, bf16[352,2048]{1,0:T(8,128)(2,1)S(1)}, u32[]{:S(2)}, u32[]{:S(2)}) collective-permute-start(bf16[352,2048]{1,0:T(8,128)(2,1)S(1)} %collective-permute-done.15.refs_7_), channel_id=1, source_target_pairs={{0,8},{1,25},{2,10},{3,27},{4,12},{5,29},{6,14},{7,31},{8,0},{9,17... | collective-permute-start | bytes 4325384 | tf_op jit(solution)/shard_map/ppermute | solution.py:52
  92.1 1.6 copy-start.4
  92.1 8.8 %copy-start = (bf16[64,2048]{1,0:T(8,128)(2,1)S(1)}, bf16[64,2048]{1,0:T(8,128)(2,1)}, u32[]{:S(2)}) copy-start(bf16[64,2048]{1,0:T(8,128)(2,1)} %hidden.3) | copy-start | bytes 786436
  92.1 8.8 %copy-start.2 = (f32[2048]{0:T(1024)S(1)}, f32[2048]{0:T(1024)}, u32[]{:S(2)}) copy-start(f32[2048]{0:T(1024)} %param.24) | copy-start | bytes 24580
  92.2 8.8 %copy-start.3 = (s32[64,2]{0,1:T(2,128)S(1)}, s32[64,2]{0,1:T(2,128)}, u32[]{:S(2)}) copy-start(s32[64,2]{0,1:T(2,128)} %param.17) | copy-start | bytes 1540
  93.7 53.3 %collective-permute-start.12 = (bf16[528,2048]{1,0:T(8,128)(2,1)S(1)}, bf16[528,2048]{1,0:T(8,128)(2,1)S(1)}, u32[]{:S(2)}, u32[]{:S(2)}) collective-permute-start(bf16[528,2048]{1,0:T(8,128)(2,1)S(1)} %slice.31), channel_id=1, source_target_pairs={{0,96},{1,33},{2,98},{3,35},{4,100},{5,37},{6,102},{7,39},{8,104},... | collective-permute-start | bytes 6488072 | tf_op jit(solution)/shard_map/ppermute | solution.py:52
  95.1 5.8 %collective-permute-start.9 = (bf16[64,2048]{1,0:T(8,128)(2,1)S(1)}, bf16[64,2048]{1,0:T(8,128)(2,1)S(1)}, u32[]{:S(2)}, u32[]{:S(2)}) collective-permute-start(bf16[64,2048]{1,0:T(8,128)(2,1)S(1)} %add_convert_fusion.2), channel_id=1, source_target_pairs={{0,6},{1,3},{2,4},{3,1},{4,2},{5,7},{6,0},{7,5},{8,14},{9,11},{10,... | collective-permute-start | bytes 786440 | tf_op jit(solution)/shard_map/ppermute | solution.py:56
  123.6 27.7 %collective-permute-start.17 = (bf16[192,2048]{1,0:T(8,128)(2,1)S(1)}, bf16[192,2048]{1,0:T(8,128)(2,1)S(1)}, u32[]{:S(2)}, u32[]{:S(2)}) collective-permute-start(bf16[192,2048]{1,0:T(8,128)(2,1)S(1)} %bitcast.16), channel_id=1, source_target_pairs={{0,56},{1,105},{2,58},{3,107},{4,60},{5,109},{6,62},{7,111},{8,48}... | collective-permute-start | bytes 2359304 | tf_op jit(solution)/shard_map/ppermute | solution.py:52
  123.6 32.9 %collective-permute-start.19 = (bf16[192,2048]{1,0:T(8,128)(2,1)S(1)}, bf16[192,2048]{1,0:T(8,128)(2,1)S(1)}, u32[]{:S(2)}, u32[]{:S(2)}) collective-permute-start(bf16[192,2048]{1,0:T(8,128)(2,1)S(1)} %bitcast.17), channel_id=1, source_target_pairs={{0,24},{1,9},{2,26},{3,11},{4,28},{5,13},{6,30},{7,15},{8,16},{9,1... | collective-permute-start | bytes 2359304 | tf_op jit(solution)/shard_map/ppermute | solution.py:52
  124.8 22.3 %copy-start.5 = (bf16[2,352,2048]{2,1,0:T(8,128)(2,1)}, bf16[2,352,2048]{2,1,0:T(8,128)(2,1)S(1)}, u32[]{:S(2)}) copy-start(bf16[2,352,2048]{2,1,0:T(8,128)(2,1)S(1)} %collective-permute-done.11.refs_2_) | copy-start | bytes 8650756
  124.8 38.4 %collective-permute-start.21 = (bf16[192,2048]{1,0:T(8,128)(2,1)S(1)}, bf16[192,2048]{1,0:T(8,128)(2,1)S(1)}, u32[]{:S(2)}, u32[]{:S(2)}) collective-permute-start(bf16[192,2048]{1,0:T(8,128)(2,1)S(1)} %bitcast.18), channel_id=1, source_target_pairs={{0,32},{1,97},{2,34},{3,99},{4,36},{5,101},{6,38},{7,103},{8,40},{... | collective-permute-start | bytes 2359304 | tf_op jit(solution)/shard_map/ppermute | solution.py:52
  127.6 19.4 %collective-permute-start.13 = (bf16[176,2048]{1,0:T(8,128)(2,1)S(1)}, bf16[176,2048]{1,0:T(8,128)(2,1)S(1)}, u32[]{:S(2)}, u32[]{:S(2)}) collective-permute-start(bf16[176,2048]{1,0:T(8,128)(2,1)S(1)} %slice.32), channel_id=1, source_target_pairs={{0,8},{1,25},{2,10},{3,27},{4,12},{5,29},{6,14},{7,31},{8,0},{9,17... | collective-permute-start | bytes 2162696 | tf_op jit(solution)/shard_map/ppermute | solution.py:52
  156.4 19.8 %collective-permute-start.18 = (bf16[192,2048]{1,0:T(8,128)(2,1)S(1)}, bf16[192,2048]{1,0:T(8,128)(2,1)S(1)}, u32[]{:S(2)}, u32[]{:S(2)}) collective-permute-start(bf16[192,2048]{1,0:T(8,128)(2,1)S(1)} %shard_map.137), channel_id=1, source_target_pairs={{0,56},{1,105},{2,58},{3,107},{4,60},{5,109},{6,62},{7,111},{8,48}... | collective-permute-start | bytes 2359304 | tf_op jit(solution)/shard_map/ppermute | solution.py:52
  161.7 14.5 %collective-permute-start.20 = (bf16[192,2048]{1,0:T(8,128)(2,1)S(1)}, bf16[192,2048]{1,0:T(8,128)(2,1)S(1)}, u32[]{:S(2)}, u32[]{:S(2)}) collective-permute-start(bf16[192,2048]{1,0:T(8,128)(2,1)S(1)} %shard_map.138), channel_id=1, source_target_pairs={{0,24},{1,9},{2,26},{3,11},{4,28},{5,13},{6,30},{7,15},{8,16},{9,1... | collective-permute-start | bytes 2359304 | tf_op jit(solution)/shard_map/ppermute | solution.py:52
  168.3 12.1 %collective-permute-start.22 = (bf16[192,2048]{1,0:T(8,128)(2,1)S(1)}, bf16[192,2048]{1,0:T(8,128)(2,1)S(1)}, u32[]{:S(2)}, u32[]{:S(2)}) collective-permute-start(bf16[192,2048]{1,0:T(8,128)(2,1)S(1)} %shard_map.139), channel_id=1, source_target_pairs={{0,32},{1,97},{2,34},{3,99},{4,36},{5,101},{6,38},{7,103},{8,40},{... | collective-permute-start | bytes 2359304 | tf_op jit(solution)/shard_map/ppermute | solution.py:52
  181.9 6.5 %copy-start.1 = (f32[2048,8]{0,1:T(8,128)S(1)}, f32[2048,8]{0,1:T(8,128)}, u32[]{:S(2)}) copy-start(f32[2048,8]{0,1:T(8,128)} %param.25) | copy-start | bytes 196612
  181.9 18.7 %all-to-all-start.1 = ((bf16[8,24,2048]{2,1,0:T(8,128)(2,1)}), bf16[8,24,2048]{2,1,0:T(8,128)(2,1)S(1)}, u32[]{:S(2)}, u32[]{:S(2)}) async-start(bf16[8,24,2048]{2,1,0:T(8,128)(2,1)} %bitcast.14), calls=%async_computation.1 | async-start | bytes 1572864 | tf_op jit(solution)/shard_map/all_to_all | solution.py:498

commit v2 on v1

--- a/solution.py
+++ b/solution.py
@@ -1,3 +1,4 @@
+import functools
 import math
 
 import jax
@@ -407,28 +408,37 @@
     )(*gus, *downs)
 
 
-def expert_body(rows, weights, out, act_s):
-    x = rows[...]
+def expert_body(count, *refs):
+    weights, outs = refs[count], refs[count + 1 : 2 * count + 1]
+    act_s = refs[-1]
+    if count == 1:
+        x = refs[0][...]
+    else:
+        x = jnp.concatenate([ref[...] for ref in refs[:count]], axis=0)
     for lo in range(0, FF4, 256):
         hi = min(lo + 256, FF4)
         gate = matmul_t(x, weights[lo:hi, :])
         up = matmul_t(x, weights[FF4 + lo : FF4 + hi, :])
         act_s[:, lo:hi] = (gate / (1.0 + jnp.exp(-gate)) * up).astype(BF)
     act = act_s[...]
+    size = 8 * SLOTS
     for lo in range(0, D, 256):
-        out[:, lo : lo + 256] = matmul(act, weights[2 * FF4 :, lo : lo + 256]).astype(BF)
-
-
-def experts(rows, weights):
+        result = matmul(act, weights[2 * FF4 :, lo : lo + 256]).astype(BF)
+        for i, out in enumerate(outs):
+            out[:, lo : lo + 256] = result[i * size : (i + 1) * size]
+
+
+def experts(blocks, weights):
     vmem = pl.BlockSpec(memory_space=pltpu.VMEM)
-    return pl.pallas_call(
-        expert_body,
-        in_specs=[vmem] * 2,
-        out_specs=vmem,
-        out_shape=jax.ShapeDtypeStruct(rows.shape, BF),
-        scratch_shapes=[pltpu.VMEM((rows.shape[0], FF4), BF)],
-        compiler_params=pltpu.CompilerParams(vmem_limit_bytes=8 << 20),
-    )(rows, weights)
+    count = len(blocks)
+    return pl.pallas_call(
+        functools.partial(expert_body, count),
+        in_specs=[vmem] * (count + 1),
+        out_specs=[vmem] * count,
+        out_shape=[jax.ShapeDtypeStruct((8 * SLOTS, D), BF)] * count,
+        scratch_shapes=[pltpu.VMEM((count * 8 * SLOTS, FF4), BF)],
+        compiler_params=pltpu.CompilerParams(vmem_limit_bytes=12 << 20),
+    )(*blocks, weights)
 
 
 def in_hbm(array):
@@ -486,13 +496,12 @@
     x_d = send_xy(x_own, TXY)
     x_x = send_xy(x_own, TX)
     x_y = send_xy(x_own, TY)
-    part = experts(x_own, weights)
-    part_d = experts(x_d, weights)
+    (part_d,) = experts([x_d], weights)
     got_d = send_xy(part_d, TXY)
-    part_x = experts(x_x, weights)
+    part_x, part_y = experts([x_x, x_y], weights)
     got_x = send_xy(part_x, TX)
-    part_y = experts(x_y, weights)
     got_y = send_xy(part_y, TY)
+    (part,) = experts([x_own], weights)
     rows = part.astype(F32) + got_d.astype(F32) + got_x.astype(F32) + got_y.astype(F32)
     rows = rows.astype(BF).reshape(8, SLOTS, D)
     returned = lax.all_to_all(rows, "head", split_axis=0, concat_axis=0, tiled=True)

time: 202 us -> 199 us (0.985)
  Pallas kernels: 47.1 us -> 44.3 us
    pallas_call x4 -> x3, Pallas kernels: 20.6 us -> 17.8 us  [experts(): pl.pallas_call(functools.partial(expert_body, count), in_specs=[vmem] * (...]
  transfers between devices with their start and end apart: 24 -> 24, of which waited for: 9 -> 10; matrix products, arithmetic and copies ran while one was open for 1% -> 1% of each run, Pallas kernels for 22% -> 21%
where the time goes in v2:
time: 199 us
  waiting for transfers between devices  85 us (43%)
  Pallas kernels  44.3 us (22%)
  starting transfers between devices  42.9 us (22%)
  blocking collectives  22.1 us (11%)
  other arithmetic  2.7 us (1%)
    ppermute x13, waiting for transfers between devices, send_xy(): return lax.ppermute(v, AXES, pairs)  63.8 us
    all_to_all x1, blocking collectives, per_device(): lax.all_to_all(rows.reshape(8, SLOTS, D), 'head', split_axis=0, concat_ax...  22.1 us
    ppermute x13, starting transfers between devices, send_xy(): return lax.ppermute(v, AXES, pairs)  20.5 us
    pallas_call x1, Pallas kernels, attention(): pl.pallas_call(attention_body, in_specs=[vmem] * 11 + [hbm] * 4, out_spec...  19 us
    pallas_call x3, Pallas kernels, experts(): pl.pallas_call(functools.partial(expert_body, count), in_specs=[vmem] * (...  17.8 us
    ppermute x10, starting transfers between devices, send_h(): return lax.ppermute(v, 'head', pairs)  16.5 us
    all_to_all x1, waiting for transfers between devices, per_device(): lax.all_to_all(rows, 'head', split_axis=0, concat_axis=0, tiled=True)  11.8 us
    ppermute x10, waiting for transfers between devices, send_h(): return lax.ppermute(v, 'head', pairs)  9.46 us
  transfers between devices with their start and end apart: 24, of which 10 were waited for; matrix products, arithmetic and copies ran while one was open for 1% of the time, Pallas kernels for 21%

profile of v2, /device:TPU:1, one launch (start us, length us, event | category | flops | bytes accessed | tf_op | source)
XLA Modules:
  0.0 198.9 jit_solution(11851686484272391152)
XLA Ops:
  0.0 1.1 prepare.1.c0
  1.1 4.7 %collective-permute-start = (bf16[64,2176]{1,0:T(8,128)(2,1)S(1)}, bf16[64,2176]{1,0:T(8,128)(2,1)S(1)}, u32[]{:S(2)}, u32[]{:S(2)}) collective-permute-start(bf16[64,2176]{1,0:T(8,128)(2,1)S(1)} %prepare.1.c0), channel_id=1, source_target_pairs={{0,2},{1,7},{2,0},{3,5},{4,6},{5,3},{6,4},{7,1},{8,10},{9,15},{10,... | collective-permute-start | bytes 835592 | tf_op jit(solution)/shard_map/ppermute | solution.py:57
  5.8 2.5 %collective-permute-start.10 = (bf16[2,352,2048]{2,1,0:T(8,128)(2,1)}, bf16[2,352,2048]{2,1,0:T(8,128)(2,1)S(1)}, u32[]{:S(2)}, u32[]{:S(2)}) collective-permute-start(bf16[2,352,2048]{2,1,0:T(8,128)(2,1)} %bitcast.29), channel_id=1, source_target_pairs={{0,8},{1,25},{2,10},{3,27},{4,12},{5,29},{6,14},{7,31},{8,0},{9,17... | collective-permute-start | bytes 8650760 | tf_op jit(solution)/shard_map/ppermute | solution.py:53
  8.3 0.0 collective-permute-start.1
  8.3 1.5 collective-permute-done.c1
  9.7 0.0 collective-permute-start.2
  9.7 5.1 %collective-permute-start.3 = (bf16[64,2176]{1,0:T(8,128)(2,1)S(1)}, bf16[64,2176]{1,0:T(8,128)(2,1)S(1)}, u32[]{:S(2)}, u32[]{:S(2)}) collective-permute-start(bf16[64,2176]{1,0:T(8,128)(2,1)S(1)} %prepare.1.c0), channel_id=1, source_target_pairs={{0,1},{1,0},{2,3},{3,2},{4,5},{5,4},{6,7},{7,6},{8,9},{9,8},{10,11... | collective-permute-start | bytes 835592 | tf_op jit(solution)/shard_map/ppermute | solution.py:57
  14.9 0.1 collective-permute-start.4
  14.9 0.0 collective-permute-done.1.c2
  14.9 0.4 collective-permute-start.5
  15.4 1.6 collective-permute-done.2.c3
  16.9 2.4 %collective-permute-start.6 = (bf16[64,2176]{1,0:T(8,128)(2,1)S(1)}, bf16[64,2176]{1,0:T(8,128)(2,1)S(1)}, u32[]{:S(2)}, u32[]{:S(2)}) collective-permute-start(bf16[64,2176]{1,0:T(8,128)(2,1)S(1)} %collective-permute-done.2.c3), channel_id=1, source_target_pairs={{0,1},{1,0},{2,3},{3,2},{4,5},{5,4},{6,7},{7,6},{8,9},{9,8},{10,11... | collective-permute-start | bytes 835592 | tf_op jit(solution)/shard_map/ppermute | solution.py:57
  19.4 0.1 pad_maximum_fusion
  19.4 1.0 fusion
  20.4 0.0 collective-permute-done.3.c4
  20.4 0.0 collective-permute-done.4.c5
  20.4 0.0 collective-permute-done.5.c6
  20.5 0.1 collective-permute-done.6.c7
  20.6 19.0 %attention.1 = (bf16[256,2048]{1,0:T(8,128)(2,1)S(1)}, bf16[256,2048]{1,0:T(8,128)(2,1)S(1)}) custom-call(bf16[64,2176]{1,0:T(8,128)(2,1)S(1)} %prepare.1.c0, bf16[64,2176]{1,0:T(8,128)(2,1)S(1)} %collective-permute-done.c1, bf16[64,2176]{1,0:T(8,128)(2,1)S(1)} %collective-permute-done.1.c2, bf16[64,2176]{1,0:T(8,128)(2,1)S(1)} %collective-permute-done.2.c3, ...), custom_call_target="tpu_custom_call" | custom-call | tf_op jit(solution)/shard_map/attention/pallas_call | solution.py:239
  39.5 0.5 collective-permute-start.7
  40.0 1.3 collective-permute-start.11
  41.3 0.2 collective-permute-start.15
  41.5 0.8 collective-permute-done.7.got
  42.3 0.1 add_convert_fusion.1
  42.4 3.0 %collective-permute-start.8 = (bf16[128,2048]{1,0:T(8,128)(2,1)S(1)}, bf16[128,2048]{1,0:T(8,128)(2,1)S(1)}, u32[]{:S(2)}, u32[]{:S(2)}) collective-permute-start(bf16[128,2048]{1,0:T(8,128)(2,1)S(1)} %add_convert_fusion.1), channel_id=1, source_target_pairs={{0,2},{1,7},{2,0},{3,5},{4,6},{5,3},{6,4},{7,1},{8,10},{9,15},{10,... | collective-permute-start | bytes 1572872 | tf_op jit(solution)/shard_map/ppermute | solution.py:57
  45.5 3.1 %collective-permute-start.14 = (bf16[352,2048]{1,0:T(8,128)(2,1)S(1)}, bf16[352,2048]{1,0:T(8,128)(2,1)S(1)}, u32[]{:S(2)}, u32[]{:S(2)}) collective-permute-start(bf16[352,2048]{1,0:T(8,128)(2,1)S(1)} %bitcast.34), channel_id=1, source_target_pairs={{0,8},{1,25},{2,10},{3,27},{4,12},{5,29},{6,14},{7,31},{8,0},{9,17... | collective-permute-start | bytes 4325384 | tf_op jit(solution)/shard_map/ppermute | solution.py:53
  48.5 40.5 %collective-permute-done.15.refs_7_ = bf16[352,2048]{1,0:T(8,128)(2,1)S(1)} collective-permute-done((bf16[352,2048]{1,0:T(8,128)(2,1)S(1)}, bf16[352,2048]{1,0:T(8,128)(2,1)S(1)}, u32[]{:S(2)}, u32[]{:S(2)}) %collective-permute-start.15) | collective-permute-done | bytes 1441824 | tf_op jit(solution)/shard_map/ppermute | solution.py:53
  89.1 3.1 %collective-permute-start.16 = (bf16[352,2048]{1,0:T(8,128)(2,1)S(1)}, bf16[352,2048]{1,0:T(8,128)(2,1)S(1)}, u32[]{:S(2)}, u32[]{:S(2)}) collective-permute-start(bf16[352,2048]{1,0:T(8,128)(2,1)S(1)} %collective-permute-done.15.refs_7_), channel_id=1, source_target_pairs={{0,8},{1,25},{2,10},{3,27},{4,12},{5,29},{6,14},{7,31},{8,0},{9,17... | collective-permute-start | bytes 4325384 | tf_op jit(solution)/shard_map/ppermute | solution.py:53
  92.1 0.0 collective-permute-done.10.refs_1_
  92.2 0.0 copy-start.3
  92.2 0.2 slice.31
  92.4 1.3 copy-done.4
  93.7 1.3 collective-permute-start.12
  95.0 0.0 collective-permute-done.8.got_a
  95.0 0.1 add_convert_fusion.2
  95.1 0.3 collective-permute-start.9
  95.4 5.5 %collective-permute-done.9.got_b = bf16[64,2048]{1,0:T(8,128)(2,1)S(1)} collective-permute-done((bf16[64,2048]{1,0:T(8,128)(2,1)S(1)}, bf16[64,2048]{1,0:T(8,128)(2,1)S(1)}, u32[]{:S(2)}, u32[]{:S(2)}) %collective-permute-start.9) | collective-permute-done | bytes 262176 | tf_op jit(solution)/shard_map/ppermute | solution.py:57
  100.9 0.6 settle.1
  101.5 22.1 %all_to_all.10 = bf16[8,24,2048]{2,1,0:T(8,128)(2,1)S(1)} all-to-all(bf16[8,24,2048]{2,1,0:T(8,128)(2,1)S(1)} %bitcast.21), channel_id=1, replica_groups=mesh['req'=16,'head'=8] {'head'}, dimensions={0} | all-to-all | bytes 1572864 | tf_op jit(solution)/shard_map/all_to_all | solution.py:492
  123.6 0.0 collective-permute-start.17
  123.6 0.0 collective-permute-done.14.refs_6_
  123.6 1.1 collective-permute-start.19
  124.8 0.0 collective-permute-done.11.refs_2_
  124.8 2.7 %collective-permute-start.20 = (bf16[192,2048]{1,0:T(8,128)(2,1)S(1)}, bf16[192,2048]{1,0:T(8,128)(2,1)S(1)}, u32[]{:S(2)}, u32[]{:S(2)}) collective-permute-start(bf16[192,2048]{1,0:T(8,128)(2,1)S(1)} %bitcast.18), channel_id=1, source_target_pairs={{0,32},{1,97},{2,34},{3,99},{4,36},{5,101},{6,38},{7,103},{8,40},{... | collective-permute-start | bytes 2359304 | tf_op jit(solution)/shard_map/ppermute | solution.py:53
  127.5 0.1 slice.32
  127.6 0.0 collective-permute-done.16.refs_8_
  127.6 1.3 collective-permute-start.13
  128.9 18.2 %collective-permute-done.13.refs_4_ = bf16[176,2048]{1,0:T(8,128)(2,1)S(1)} collective-permute-done((bf16[176,2048]{1,0:T(8,128)(2,1)S(1)}, bf16[176,2048]{1,0:T(8,128)(2,1)S(1)}, u32[]{:S(2)}, u32[]{:S(2)}) %collective-permute-start.13) | collective-permute-done | bytes 720928 | tf_op jit(solution)/shard_map/ppermute | solution.py:53
  147.0 4.2 %pack.1.refs_1_.refs_2_ = bf16[4224,2048]{1,0:T(8,128)(2,1)S(1)} custom-call(bf16[2,352,2048]{2,1,0:T(8,128)(2,1)} %bitcast.30, bf16[2,352,2048]{2,1,0:T(8,128)(2,1)} %copy-done.4, bf16[2,352,2048]{2,1,0:T(8,128)(2,1)} %copy-done.5, bf16[528,2048]{1,0:T(8,128)(2,1)S(1)} %collective-permute-done.12.refs_3_, ...), custom_call_target="tpu_custom_call" | custom-call | tf_op jit(solution)/shard_map/pack/pallas_call | solution.py:400
  151.3 0.0 collective-permute-done.17.refs_0_
  151.3 5.1 %shard_map.137 = bf16[192,2048]{1,0:T(8,128)(2,1)S(1)} custom-call(bf16[192,2048]{1,0:T(8,128)(2,1)S(1)} %collective-permute-done.17.refs_0_, bf16[4224,2048]{1,0:T(8,128)(2,1)S(1)} %pack.1.refs_1_.refs_2_), custom_call_target="tpu_custom_call" | custom-call | tf_op jit(solution)/shard_map/pallas_call | solution.py:434
  156.4 0.1 collective-permute-start.18
  156.5 0.0 collective-permute-done.19.refs_0_
  156.6 7.5 %shard_map.138 = (bf16[192,2048]{1,0:T(8,128)(2,1)S(1)}, bf16[192,2048]{1,0:T(8,128)(2,1)S(1)}) custom-call(bf16[192,2048]{1,0:T(8,128)(2,1)S(1)} %collective-permute-done.19.refs_0_, bf16[192,2048]{1,0:T(8,128)(2,1)S(1)} %collective-permute-done.20.refs_1_, bf16[4224,2048]{1,0:T(8,128)(2,1)S(1)} %pack.1.refs_1_.refs_2_), custom_call_target="tpu_custom_call" | custom-call | tf_op jit(solution)/shard_map/pallas_call | solution.py:434
  164.1 1.2 collective-permute-start.21
  165.3 2.7 %collective-permute-start.22 = (bf16[192,2048]{1,0:T(8,128)(2,1)S(1)}, bf16[192,2048]{1,0:T(8,128)(2,1)S(1)}, u32[]{:S(2)}, u32[]{:S(2)}) collective-permute-start(bf16[192,2048]{1,0:T(8,128)(2,1)S(1)} %get-tuple-element.20), channel_id=1, source_target_pairs={{0,32},{1,97},{2,34},{3,99},{4,36},{5,101},{6,38},{7,103},{8,40},{... | collective-permute-start | bytes 2359304 | tf_op jit(solution)/shard_map/ppermute | solution.py:53
  168.0 5.1 %shard_map.136 = bf16[192,2048]{1,0:T(8,128)(2,1)S(1)} custom-call(bf16[192,2048]{1,0:T(8,128)(2,1)S(1)} %bitcast.19, bf16[4224,2048]{1,0:T(8,128)(2,1)S(1)} %pack.1.refs_1_.refs_2_), custom_call_target="tpu_custom_call" | custom-call | tf_op jit(solution)/shard_map/pallas_call | solution.py:434
  173.1 2.7 %collective-permute-done.21 = bf16[192,2048]{1,0:T(8,128)(2,1)S(1)} collective-permute-done((bf16[192,2048]{1,0:T(8,128)(2,1)S(1)}, bf16[192,2048]{1,0:T(8,128)(2,1)S(1)}, u32[]{:S(2)}, u32[]{:S(2)}) %collective-permute-start.21) | collective-permute-done | bytes 786464 | tf_op jit(solution)/shard_map/ppermute | solution.py:53
  175.8 2.4 %collective-permute-done.22 = bf16[192,2048]{1,0:T(8,128)(2,1)S(1)} collective-permute-done((bf16[192,2048]{1,0:T(8,128)(2,1)S(1)}, bf16[192,2048]{1,0:T(8,128)(2,1)S(1)}, u32[]{:S(2)}, u32[]{:S(2)}) %collective-permute-start.22) | collective-permute-done | bytes 786464 | tf_op jit(solution)/shard_map/ppermute | solution.py:53
  178.2 1.4 add_convert_fusion
  179.6 6.0 %all-to-all-start.1 = ((bf16[8,24,2048]{2,1,0:T(8,128)(2,1)}), bf16[8,24,2048]{2,1,0:T(8,128)(2,1)S(1)}, u32[]{:S(2)}, u32[]{:S(2)}) async-start(bf16[8,24,2048]{2,1,0:T(8,128)(2,1)} %bitcast.14), calls=%async_computation.1 | async-start | bytes 1572864 | tf_op jit(solution)/shard_map/all_to_all | solution.py:507
  185.6 0.4 weigh.1
  186.0 11.8 %all-to-all-done.1 = bf16[8,24,2048]{2,1,0:T(8,128)(2,1)S(1)} async-done(((bf16[8,24,2048]{2,1,0:T(8,128)(2,1)}), bf16[8,24,2048]{2,1,0:T(8,128)(2,1)S(1)}, u32[]{:S(2)}, u32[]{:S(2)}) %all-to-all-start.1) | async-done | bytes 786464 | tf_op jit(solution)/shard_map/all_to_all | solution.py:507
  197.7 1.1 finish.1
  (18 shorter events, 0.0 us)
Async XLA Ops:
  1.1 8.6 %collective-permute-start = (bf16[64,2176]{1,0:T(8,128)(2,1)S(1)}, bf16[64,2176]{1,0:T(8,128)(2,1)S(1)}, u32[]{:S(2)}, u32[]{:S(2)}) collective-permute-start(bf16[64,2176]{1,0:T(8,128)(2,1)S(1)} %prepare.1.c0), channel_id=1, source_target_pairs={{0,2},{1,7},{2,0},{3,5},{4,6},{5,3},{6,4},{7,1},{8,10},{9,15},{10,... | collective-permute-start | bytes 835592 | tf_op jit(solution)/shard_map/ppermute | solution.py:57
  5.8 86.3 %collective-permute-start.10 = (bf16[2,352,2048]{2,1,0:T(8,128)(2,1)}, bf16[2,352,2048]{2,1,0:T(8,128)(2,1)S(1)}, u32[]{:S(2)}, u32[]{:S(2)}) collective-permute-start(bf16[2,352,2048]{2,1,0:T(8,128)(2,1)} %bitcast.29), channel_id=1, source_target_pairs={{0,8},{1,25},{2,10},{3,27},{4,12},{5,29},{6,14},{7,31},{8,0},{9,17... | collective-permute-start | bytes 8650760 | tf_op jit(solution)/shard_map/ppermute | solution.py:53
  8.3 6.7 %collective-permute-start.1 = (bf16[64,2176]{1,0:T(8,128)(2,1)S(1)}, bf16[64,2176]{1,0:T(8,128)(2,1)S(1)}, u32[]{:S(2)}, u32[]{:S(2)}) collective-permute-start(bf16[64,2176]{1,0:T(8,128)(2,1)S(1)} %prepare.1.c0), channel_id=1, source_target_pairs={{0,6},{1,3},{2,4},{3,1},{4,2},{5,7},{6,0},{7,5},{8,14},{9,11},{10,... | collective-permute-start | bytes 835592 | tf_op jit(solution)/shard_map/ppermute | solution.py:57
  9.7 7.2 %collective-permute-start.2 = (bf16[64,2176]{1,0:T(8,128)(2,1)S(1)}, bf16[64,2176]{1,0:T(8,128)(2,1)S(1)}, u32[]{:S(2)}, u32[]{:S(2)}) collective-permute-start(bf16[64,2176]{1,0:T(8,128)(2,1)S(1)} %collective-permute-done.c1), channel_id=1, source_target_pairs={{0,6},{1,3},{2,4},{3,1},{4,2},{5,7},{6,0},{7,5},{8,14},{9,11},{10,... | collective-permute-start | bytes 835592 | tf_op jit(solution)/shard_map/ppermute | solution.py:57
  9.7 10.7 %collective-permute-start.3 = (bf16[64,2176]{1,0:T(8,128)(2,1)S(1)}, bf16[64,2176]{1,0:T(8,128)(2,1)S(1)}, u32[]{:S(2)}, u32[]{:S(2)}) collective-permute-start(bf16[64,2176]{1,0:T(8,128)(2,1)S(1)} %prepare.1.c0), channel_id=1, source_target_pairs={{0,1},{1,0},{2,3},{3,2},{4,5},{5,4},{6,7},{7,6},{8,9},{9,8},{10,11... | collective-permute-start | bytes 835592 | tf_op jit(solution)/shard_map/ppermute | solution.py:57
  14.9 5.6 %collective-permute-start.4 = (bf16[64,2176]{1,0:T(8,128)(2,1)S(1)}, bf16[64,2176]{1,0:T(8,128)(2,1)S(1)}, u32[]{:S(2)}, u32[]{:S(2)}) collective-permute-start(bf16[64,2176]{1,0:T(8,128)(2,1)S(1)} %collective-permute-done.c1), channel_id=1, source_target_pairs={{0,1},{1,0},{2,3},{3,2},{4,5},{5,4},{6,7},{7,6},{8,9},{9,8},{10,11... | collective-permute-start | bytes 835592 | tf_op jit(solution)/shard_map/ppermute | solution.py:57
  14.9 5.5 %collective-permute-start.5 = (bf16[64,2176]{1,0:T(8,128)(2,1)S(1)}, bf16[64,2176]{1,0:T(8,128)(2,1)S(1)}, u32[]{:S(2)}, u32[]{:S(2)}) collective-permute-start(bf16[64,2176]{1,0:T(8,128)(2,1)S(1)} %collective-permute-done.1.c2), channel_id=1, source_target_pairs={{0,1},{1,0},{2,3},{3,2},{4,5},{5,4},{6,7},{7,6},{8,9},{9,8},{10,11... | collective-permute-start | bytes 835592 | tf_op jit(solution)/shard_map/ppermute | solution.py:57
  16.9 3.6 %collective-permute-start.6 = (bf16[64,2176]{1,0:T(8,128)(2,1)S(1)}, bf16[64,2176]{1,0:T(8,128)(2,1)S(1)}, u32[]{:S(2)}, u32[]{:S(2)}) collective-permute-start(bf16[64,2176]{1,0:T(8,128)(2,1)S(1)} %collective-permute-done.2.c3), channel_id=1, source_target_pairs={{0,1},{1,0},{2,3},{3,2},{4,5},{5,4},{6,7},{7,6},{8,9},{9,8},{10,11... | collective-permute-start | bytes 835592 | tf_op jit(solution)/shard_map/ppermute | solution.py:57
  20.6 19.4 %copy-start.6 = (bf16[1,2048,2,352]{1,3,2,0:T(8,128)(2,1)S(1)}, bf16[1,2048,2,352]{1,3,2,0:T(8,128)(2,1)}, u32[]{:S(2)}) copy-start(bf16[1,2048,2,352]{1,3,2,0:T(8,128)(2,1)} %param.26) | copy-start | bytes 8650756
  20.6 20.7 %copy-start.7 = (bf16[1,352,2048]{2,1,0:T(8,128)(2,1)S(1)}, bf16[1,352,2048]{2,1,0:T(8,128)(2,1)}, u32[]{:S(2)}) copy-start(bf16[1,352,2048]{2,1,0:T(8,128)(2,1)} %param.27) | copy-start | bytes 4325380
  39.5 2.7 %collective-permute-start.7 = (bf16[256,2048]{1,0:T(8,128)(2,1)S(1)}, bf16[256,2048]{1,0:T(8,128)(2,1)S(1)}, u32[]{:S(2)}, u32[]{:S(2)}) collective-permute-start(bf16[256,2048]{1,0:T(8,128)(2,1)S(1)} %get-tuple-element.14), channel_id=1, source_target_pairs={{0,1},{1,0},{2,3},{3,2},{4,5},{5,4},{6,7},{7,6},{8,9},{9,8},{10,11... | collective-permute-start | bytes 3145736 | tf_op jit(solution)/shard_map/ppermute | solution.py:57
  40.0 84.8 %collective-permute-start.11 = (bf16[2,352,2048]{2,1,0:T(8,128)(2,1)S(1)}, bf16[2,352,2048]{2,1,0:T(8,128)(2,1)S(1)}, u32[]{:S(2)}, u32[]{:S(2)}) collective-permute-start(bf16[2,352,2048]{2,1,0:T(8,128)(2,1)S(1)} %bitcast.31), channel_id=1, source_target_pairs={{0,96},{1,33},{2,98},{3,35},{4,100},{5,37},{6,102},{7,39},{8,104},... | collective-permute-start | bytes 8650760 | tf_op jit(solution)/shard_map/ppermute | solution.py:53
  41.3 47.8 %collective-permute-start.15 = (bf16[352,2048]{1,0:T(8,128)(2,1)S(1)}, bf16[352,2048]{1,0:T(8,128)(2,1)S(1)}, u32[]{:S(2)}, u32[]{:S(2)}) collective-permute-start(bf16[352,2048]{1,0:T(8,128)(2,1)S(1)} %bitcast.33), channel_id=1, source_target_pairs={{0,96},{1,33},{2,98},{3,35},{4,100},{5,37},{6,102},{7,39},{8,104},... | collective-permute-start | bytes 4325384 | tf_op jit(solution)/shard_map/ppermute | solution.py:53
  42.4 52.6 %collective-permute-start.8 = (bf16[128,2048]{1,0:T(8,128)(2,1)S(1)}, bf16[128,2048]{1,0:T(8,128)(2,1)S(1)}, u32[]{:S(2)}, u32[]{:S(2)}) collective-permute-start(bf16[128,2048]{1,0:T(8,128)(2,1)S(1)} %add_convert_fusion.1), channel_id=1, source_target_pairs={{0,2},{1,7},{2,0},{3,5},{4,6},{5,3},{6,4},{7,1},{8,10},{9,15},{10,... | collective-permute-start | bytes 1572872 | tf_op jit(solution)/shard_map/ppermute | solution.py:57
  45.5 78.2 %collective-permute-start.14 = (bf16[352,2048]{1,0:T(8,128)(2,1)S(1)}, bf16[352,2048]{1,0:T(8,128)(2,1)S(1)}, u32[]{:S(2)}, u32[]{:S(2)}) collective-permute-start(bf16[352,2048]{1,0:T(8,128)(2,1)S(1)} %bitcast.34), channel_id=1, source_target_pairs={{0,8},{1,25},{2,10},{3,27},{4,12},{5,29},{6,14},{7,31},{8,0},{9,17... | collective-permute-start | bytes 4325384 | tf_op jit(solution)/shard_map/ppermute | solution.py:53
  89.1 38.5 %collective-permute-start.16 = (bf16[352,2048]{1,0:T(8,128)(2,1)S(1)}, bf16[352,2048]{1,0:T(8,128)(2,1)S(1)}, u32[]{:S(2)}, u32[]{:S(2)}) collective-permute-start(bf16[352,2048]{1,0:T(8,128)(2,1)S(1)} %collective-permute-done.15.refs_7_), channel_id=1, source_target_pairs={{0,8},{1,25},{2,10},{3,27},{4,12},{5,29},{6,14},{7,31},{8,0},{9,17... | collective-permute-start | bytes 4325384 | tf_op jit(solution)/shard_map/ppermute | solution.py:53
  92.1 1.6 copy-start.4
  92.1 8.8 %copy-start = (bf16[64,2048]{1,0:T(8,128)(2,1)S(1)}, bf16[64,2048]{1,0:T(8,128)(2,1)}, u32[]{:S(2)}) copy-start(bf16[64,2048]{1,0:T(8,128)(2,1)} %hidden.3) | copy-start | bytes 786436
  92.1 8.8 %copy-start.2 = (f32[2048]{0:T(1024)S(1)}, f32[2048]{0:T(1024)}, u32[]{:S(2)}) copy-start(f32[2048]{0:T(1024)} %param.24) | copy-start | bytes 24580
  92.2 8.7 %copy-start.3 = (s32[64,2]{0,1:T(2,128)S(1)}, s32[64,2]{0,1:T(2,128)}, u32[]{:S(2)}) copy-start(s32[64,2]{0,1:T(2,128)} %param.17) | copy-start | bytes 1540
  93.7 53.3 %collective-permute-start.12 = (bf16[528,2048]{1,0:T(8,128)(2,1)S(1)}, bf16[528,2048]{1,0:T(8,128)(2,1)S(1)}, u32[]{:S(2)}, u32[]{:S(2)}) collective-permute-start(bf16[528,2048]{1,0:T(8,128)(2,1)S(1)} %slice.31), channel_id=1, source_target_pairs={{0,96},{1,33},{2,98},{3,35},{4,100},{5,37},{6,102},{7,39},{8,104},... | collective-permute-start | bytes 6488072 | tf_op jit(solution)/shard_map/ppermute | solution.py:53
  95.1 5.8 %collective-permute-start.9 = (bf16[64,2048]{1,0:T(8,128)(2,1)S(1)}, bf16[64,2048]{1,0:T(8,128)(2,1)S(1)}, u32[]{:S(2)}, u32[]{:S(2)}) collective-permute-start(bf16[64,2048]{1,0:T(8,128)(2,1)S(1)} %add_convert_fusion.2), channel_id=1, source_target_pairs={{0,6},{1,3},{2,4},{3,1},{4,2},{5,7},{6,0},{7,5},{8,14},{9,11},{10,... | collective-permute-start | bytes 786440 | tf_op jit(solution)/shard_map/ppermute | solution.py:57
  123.6 27.7 %collective-permute-start.17 = (bf16[192,2048]{1,0:T(8,128)(2,1)S(1)}, bf16[192,2048]{1,0:T(8,128)(2,1)S(1)}, u32[]{:S(2)}, u32[]{:S(2)}) collective-permute-start(bf16[192,2048]{1,0:T(8,128)(2,1)S(1)} %bitcast.16), channel_id=1, source_target_pairs={{0,56},{1,105},{2,58},{3,107},{4,60},{5,109},{6,62},{7,111},{8,48}... | collective-permute-start | bytes 2359304 | tf_op jit(solution)/shard_map/ppermute | solution.py:53
  123.6 32.9 %collective-permute-start.19 = (bf16[192,2048]{1,0:T(8,128)(2,1)S(1)}, bf16[192,2048]{1,0:T(8,128)(2,1)S(1)}, u32[]{:S(2)}, u32[]{:S(2)}) collective-permute-start(bf16[192,2048]{1,0:T(8,128)(2,1)S(1)} %bitcast.17), channel_id=1, source_target_pairs={{0,24},{1,9},{2,26},{3,11},{4,28},{5,13},{6,30},{7,15},{8,16},{9,1... | collective-permute-start | bytes 2359304 | tf_op jit(solution)/shard_map/ppermute | solution.py:53
  124.8 22.3 %copy-start.5 = (bf16[2,352,2048]{2,1,0:T(8,128)(2,1)}, bf16[2,352,2048]{2,1,0:T(8,128)(2,1)S(1)}, u32[]{:S(2)}) copy-start(bf16[2,352,2048]{2,1,0:T(8,128)(2,1)S(1)} %collective-permute-done.11.refs_2_) | copy-start | bytes 8650756
  124.8 31.8 %collective-permute-start.20 = (bf16[192,2048]{1,0:T(8,128)(2,1)S(1)}, bf16[192,2048]{1,0:T(8,128)(2,1)S(1)}, u32[]{:S(2)}, u32[]{:S(2)}) collective-permute-start(bf16[192,2048]{1,0:T(8,128)(2,1)S(1)} %bitcast.18), channel_id=1, source_target_pairs={{0,32},{1,97},{2,34},{3,99},{4,36},{5,101},{6,38},{7,103},{8,40},{... | collective-permute-start | bytes 2359304 | tf_op jit(solution)/shard_map/ppermute | solution.py:53
  127.6 19.4 %collective-permute-start.13 = (bf16[176,2048]{1,0:T(8,128)(2,1)S(1)}, bf16[176,2048]{1,0:T(8,128)(2,1)S(1)}, u32[]{:S(2)}, u32[]{:S(2)}) collective-permute-start(bf16[176,2048]{1,0:T(8,128)(2,1)S(1)} %slice.32), channel_id=1, source_target_pairs={{0,8},{1,25},{2,10},{3,27},{4,12},{5,29},{6,14},{7,31},{8,0},{9,17... | collective-permute-start | bytes 2162696 | tf_op jit(solution)/shard_map/ppermute | solution.py:53
  156.4 16.7 %collective-permute-start.18 = (bf16[192,2048]{1,0:T(8,128)(2,1)S(1)}, bf16[192,2048]{1,0:T(8,128)(2,1)S(1)}, u32[]{:S(2)}, u32[]{:S(2)}) collective-permute-start(bf16[192,2048]{1,0:T(8,128)(2,1)S(1)} %shard_map.137), channel_id=1, source_target_pairs={{0,56},{1,105},{2,58},{3,107},{4,60},{5,109},{6,62},{7,111},{8,48}... | collective-permute-start | bytes 2359304 | tf_op jit(solution)/shard_map/ppermute | solution.py:53
  164.1 11.7 %collective-permute-start.21 = (bf16[192,2048]{1,0:T(8,128)(2,1)S(1)}, bf16[192,2048]{1,0:T(8,128)(2,1)S(1)}, u32[]{:S(2)}, u32[]{:S(2)}) collective-permute-start(bf16[192,2048]{1,0:T(8,128)(2,1)S(1)} %get-tuple-element.19), channel_id=1, source_target_pairs={{0,24},{1,9},{2,26},{3,11},{4,28},{5,13},{6,30},{7,15},{8,16},{9,1... | collective-permute-start | bytes 2359304 | tf_op jit(solution)/shard_map/ppermute | solution.py:53
  165.3 12.9 %collective-permute-start.22 = (bf16[192,2048]{1,0:T(8,128)(2,1)S(1)}, bf16[192,2048]{1,0:T(8,128)(2,1)S(1)}, u32[]{:S(2)}, u32[]{:S(2)}) collective-permute-start(bf16[192,2048]{1,0:T(8,128)(2,1)S(1)} %get-tuple-element.20), channel_id=1, source_target_pairs={{0,32},{1,97},{2,34},{3,99},{4,36},{5,101},{6,38},{7,103},{8,40},{... | collective-permute-start | bytes 2359304 | tf_op jit(solution)/shard_map/ppermute | solution.py:53
  179.6 6.0 %copy-start.1 = (f32[2048,8]{0,1:T(8,128)S(1)}, f32[2048,8]{0,1:T(8,128)}, u32[]{:S(2)}) copy-start(f32[2048,8]{0,1:T(8,128)} %param.25) | copy-start | bytes 196612
  179.6 18.1 %all-to-all-start.1 = ((bf16[8,24,2048]{2,1,0:T(8,128)(2,1)}), bf16[8,24,2048]{2,1,0:T(8,128)(2,1)S(1)}, u32[]{:S(2)}, u32[]{:S(2)}) async-start(bf16[8,24,2048]{2,1,0:T(8,128)(2,1)} %bitcast.14), calls=%async_computation.1 | async-start | bytes 1572864 | tf_op jit(solution)/shard_map/all_to_all | solution.py:507

commit v3 on v2

--- a/solution.py
+++ b/solution.py
@@ -161,10 +161,12 @@
         k_s[:, g * HD : (g + 1) * HD] = (
             one * rope_c[...] + pltpu.roll(one, HD // 2, 1) * rope_s[...]
         ).astype(BF)
-    for copy in query_copies:
-        copy.wait()
 
     def query_step(pair, carry):
+        for side in range(2):
+            e = 2 * pair + side
+            place = pl.ds(pl.multiple_of(e * 256, 256), 256)
+            pltpu.make_async_copy(wq.at[e], wq_s.at[:, place], sems.at[e]).wait()
         here = (2 * pair).astype(F32)
         query = matmul(x_s[...], wq_s[:, pl.ds(pl.multiple_of(pair * 512, 512), 512)])
         for j in range(2):

time: 199 us -> 198 us (level)
  no operation moved by 1% of the time
where the time goes in v3:
time: 198 us
  waiting for transfers between devices  85 us (43%)
  Pallas kernels  43.2 us (22%)
  starting transfers between devices  42.9 us (22%)
  blocking collectives  22.1 us (11%)
  other arithmetic  2.7 us (1%)
    ppermute x13, waiting for transfers between devices, send_xy(): return lax.ppermute(v, AXES, pairs)  63.8 us
    all_to_all x1, blocking collectives, per_device(): lax.all_to_all(rows.reshape(8, SLOTS, D), 'head', split_axis=0, concat_ax...  22.1 us
    ppermute x13, starting transfers between devices, send_xy(): return lax.ppermute(v, AXES, pairs)  20.5 us
    pallas_call x1, Pallas kernels, attention(): pl.pallas_call(attention_body, in_specs=[vmem] * 11 + [hbm] * 4, out_spec...  17.8 us
    pallas_call x3, Pallas kernels, experts(): pl.pallas_call(functools.partial(expert_body, count), in_specs=[vmem] * (...  17.8 us
    ppermute x10, starting transfers between devices, send_h(): return lax.ppermute(v, 'head', pairs)  16.5 us
    all_to_all x1, waiting for transfers between devices, per_device(): lax.all_to_all(rows, 'head', split_axis=0, concat_axis=0, tiled=True)  11.8 us
    ppermute x10, waiting for transfers between devices, send_h(): return lax.ppermute(v, 'head', pairs)  9.46 us
  transfers between devices with their start and end apart: 24, of which 10 were waited for; matrix products, arithmetic and copies ran while one was open for 1% of the time, Pallas kernels for 21%

profile of v3, /device:TPU:1, one launch (start us, length us, event | category | flops | bytes accessed | tf_op | source)
XLA Modules:
  0.0 197.8 jit_solution(2019584056766114888)
XLA Ops:
  0.0 1.1 prepare.1.c0
  1.1 4.7 %collective-permute-start = (bf16[64,2176]{1,0:T(8,128)(2,1)S(1)}, bf16[64,2176]{1,0:T(8,128)(2,1)S(1)}, u32[]{:S(2)}, u32[]{:S(2)}) collective-permute-start(bf16[64,2176]{1,0:T(8,128)(2,1)S(1)} %prepare.1.c0), channel_id=1, source_target_pairs={{0,2},{1,7},{2,0},{3,5},{4,6},{5,3},{6,4},{7,1},{8,10},{9,15},{10,... | collective-permute-start | bytes 835592 | tf_op jit(solution)/shard_map/ppermute | solution.py:57
  5.8 2.5 %collective-permute-start.10 = (bf16[2,352,2048]{2,1,0:T(8,128)(2,1)}, bf16[2,352,2048]{2,1,0:T(8,128)(2,1)S(1)}, u32[]{:S(2)}, u32[]{:S(2)}) collective-permute-start(bf16[2,352,2048]{2,1,0:T(8,128)(2,1)} %bitcast.29), channel_id=1, source_target_pairs={{0,8},{1,25},{2,10},{3,27},{4,12},{5,29},{6,14},{7,31},{8,0},{9,17... | collective-permute-start | bytes 8650760 | tf_op jit(solution)/shard_map/ppermute | solution.py:53
  8.3 0.0 collective-permute-start.1
  8.3 1.5 collective-permute-done.c1
  9.7 0.0 collective-permute-start.2
  9.7 5.1 %collective-permute-start.3 = (bf16[64,2176]{1,0:T(8,128)(2,1)S(1)}, bf16[64,2176]{1,0:T(8,128)(2,1)S(1)}, u32[]{:S(2)}, u32[]{:S(2)}) collective-permute-start(bf16[64,2176]{1,0:T(8,128)(2,1)S(1)} %prepare.1.c0), channel_id=1, source_target_pairs={{0,1},{1,0},{2,3},{3,2},{4,5},{5,4},{6,7},{7,6},{8,9},{9,8},{10,11... | collective-permute-start | bytes 835592 | tf_op jit(solution)/shard_map/ppermute | solution.py:57
  14.9 0.1 collective-permute-start.4
  14.9 0.0 collective-permute-done.1.c2
  14.9 0.4 collective-permute-start.5
  15.4 1.6 collective-permute-done.2.c3
  16.9 2.4 %collective-permute-start.6 = (bf16[64,2176]{1,0:T(8,128)(2,1)S(1)}, bf16[64,2176]{1,0:T(8,128)(2,1)S(1)}, u32[]{:S(2)}, u32[]{:S(2)}) collective-permute-start(bf16[64,2176]{1,0:T(8,128)(2,1)S(1)} %collective-permute-done.2.c3), channel_id=1, source_target_pairs={{0,1},{1,0},{2,3},{3,2},{4,5},{5,4},{6,7},{7,6},{8,9},{9,8},{10,11... | collective-permute-start | bytes 835592 | tf_op jit(solution)/shard_map/ppermute | solution.py:57
  19.4 0.1 pad_maximum_fusion
  19.4 1.0 fusion
  20.4 0.0 collective-permute-done.3.c4
  20.4 0.0 collective-permute-done.4.c5
  20.4 0.0 collective-permute-done.5.c6
  20.5 0.1 collective-permute-done.6.c7
  20.6 17.8 %attention.1 = (bf16[256,2048]{1,0:T(8,128)(2,1)S(1)}, bf16[256,2048]{1,0:T(8,128)(2,1)S(1)}) custom-call(bf16[64,2176]{1,0:T(8,128)(2,1)S(1)} %prepare.1.c0, bf16[64,2176]{1,0:T(8,128)(2,1)S(1)} %collective-permute-done.c1, bf16[64,2176]{1,0:T(8,128)(2,1)S(1)} %collective-permute-done.1.c2, bf16[64,2176]{1,0:T(8,128)(2,1)S(1)} %collective-permute-done.2.c3, ...), custom_call_target="tpu_custom_call" | custom-call | tf_op jit(solution)/shard_map/attention/pallas_call | solution.py:241
  38.4 0.5 collective-permute-start.7
  38.9 1.3 collective-permute-start.11
  40.2 0.2 collective-permute-start.15
  40.3 0.8 collective-permute-done.7.got
  41.2 0.1 add_convert_fusion.1
  41.3 3.0 %collective-permute-start.8 = (bf16[128,2048]{1,0:T(8,128)(2,1)S(1)}, bf16[128,2048]{1,0:T(8,128)(2,1)S(1)}, u32[]{:S(2)}, u32[]{:S(2)}) collective-permute-start(bf16[128,2048]{1,0:T(8,128)(2,1)S(1)} %add_convert_fusion.1), channel_id=1, source_target_pairs={{0,2},{1,7},{2,0},{3,5},{4,6},{5,3},{6,4},{7,1},{8,10},{9,15},{10,... | collective-permute-start | bytes 1572872 | tf_op jit(solution)/shard_map/ppermute | solution.py:57
  44.3 3.1 %collective-permute-start.14 = (bf16[352,2048]{1,0:T(8,128)(2,1)S(1)}, bf16[352,2048]{1,0:T(8,128)(2,1)S(1)}, u32[]{:S(2)}, u32[]{:S(2)}) collective-permute-start(bf16[352,2048]{1,0:T(8,128)(2,1)S(1)} %bitcast.34), channel_id=1, source_target_pairs={{0,8},{1,25},{2,10},{3,27},{4,12},{5,29},{6,14},{7,31},{8,0},{9,17... | collective-permute-start | bytes 4325384 | tf_op jit(solution)/shard_map/ppermute | solution.py:53
  47.4 40.5 %collective-permute-done.15.refs_7_ = bf16[352,2048]{1,0:T(8,128)(2,1)S(1)} collective-permute-done((bf16[352,2048]{1,0:T(8,128)(2,1)S(1)}, bf16[352,2048]{1,0:T(8,128)(2,1)S(1)}, u32[]{:S(2)}, u32[]{:S(2)}) %collective-permute-start.15) | collective-permute-done | bytes 1441824 | tf_op jit(solution)/shard_map/ppermute | solution.py:53
  87.9 3.1 %collective-permute-start.16 = (bf16[352,2048]{1,0:T(8,128)(2,1)S(1)}, bf16[352,2048]{1,0:T(8,128)(2,1)S(1)}, u32[]{:S(2)}, u32[]{:S(2)}) collective-permute-start(bf16[352,2048]{1,0:T(8,128)(2,1)S(1)} %collective-permute-done.15.refs_7_), channel_id=1, source_target_pairs={{0,8},{1,25},{2,10},{3,27},{4,12},{5,29},{6,14},{7,31},{8,0},{9,17... | collective-permute-start | bytes 4325384 | tf_op jit(solution)/shard_map/ppermute | solution.py:53
  91.0 0.0 collective-permute-done.10.refs_1_
  91.0 0.0 copy-start.3
  91.0 0.2 slice.31
  91.3 1.3 copy-done.4
  92.6 1.3 collective-permute-start.12
  93.9 0.0 collective-permute-done.8.got_a
  93.9 0.1 add_convert_fusion.2
  94.0 0.3 collective-permute-start.9
  94.3 5.5 %collective-permute-done.9.got_b = bf16[64,2048]{1,0:T(8,128)(2,1)S(1)} collective-permute-done((bf16[64,2048]{1,0:T(8,128)(2,1)S(1)}, bf16[64,2048]{1,0:T(8,128)(2,1)S(1)}, u32[]{:S(2)}, u32[]{:S(2)}) %collective-permute-start.9) | collective-permute-done | bytes 262176 | tf_op jit(solution)/shard_map/ppermute | solution.py:57
  99.8 0.6 settle.1
  100.4 22.1 %all_to_all.10 = bf16[8,24,2048]{2,1,0:T(8,128)(2,1)S(1)} all-to-all(bf16[8,24,2048]{2,1,0:T(8,128)(2,1)S(1)} %bitcast.21), channel_id=1, replica_groups=mesh['req'=16,'head'=8] {'head'}, dimensions={0} | all-to-all | bytes 1572864 | tf_op jit(solution)/shard_map/all_to_all | solution.py:494
  122.5 0.0 collective-permute-start.17
  122.5 0.0 collective-permute-done.14.refs_6_
  122.5 1.1 collective-permute-start.19
  123.6 0.0 collective-permute-done.11.refs_2_
  123.6 2.7 %collective-permute-start.20 = (bf16[192,2048]{1,0:T(8,128)(2,1)S(1)}, bf16[192,2048]{1,0:T(8,128)(2,1)S(1)}, u32[]{:S(2)}, u32[]{:S(2)}) collective-permute-start(bf16[192,2048]{1,0:T(8,128)(2,1)S(1)} %bitcast.18), channel_id=1, source_target_pairs={{0,32},{1,97},{2,34},{3,99},{4,36},{5,101},{6,38},{7,103},{8,40},{... | collective-permute-start | bytes 2359304 | tf_op jit(solution)/shard_map/ppermute | solution.py:53
  126.4 0.1 slice.32
  126.4 0.0 collective-permute-done.16.refs_8_
  126.4 1.3 collective-permute-start.13
  127.7 18.2 %collective-permute-done.13.refs_4_ = bf16[176,2048]{1,0:T(8,128)(2,1)S(1)} collective-permute-done((bf16[176,2048]{1,0:T(8,128)(2,1)S(1)}, bf16[176,2048]{1,0:T(8,128)(2,1)S(1)}, u32[]{:S(2)}, u32[]{:S(2)}) %collective-permute-start.13) | collective-permute-done | bytes 720928 | tf_op jit(solution)/shard_map/ppermute | solution.py:53
  145.9 4.2 %pack.1.refs_1_.refs_2_ = bf16[4224,2048]{1,0:T(8,128)(2,1)S(1)} custom-call(bf16[2,352,2048]{2,1,0:T(8,128)(2,1)} %bitcast.30, bf16[2,352,2048]{2,1,0:T(8,128)(2,1)} %copy-done.4, bf16[2,352,2048]{2,1,0:T(8,128)(2,1)} %copy-done.5, bf16[528,2048]{1,0:T(8,128)(2,1)S(1)} %collective-permute-done.12.refs_3_, ...), custom_call_target="tpu_custom_call" | custom-call | tf_op jit(solution)/shard_map/pack/pallas_call | solution.py:402
  150.2 5.1 %shard_map.137 = bf16[192,2048]{1,0:T(8,128)(2,1)S(1)} custom-call(bf16[192,2048]{1,0:T(8,128)(2,1)S(1)} %collective-permute-done.17.refs_0_, bf16[4224,2048]{1,0:T(8,128)(2,1)S(1)} %pack.1.refs_1_.refs_2_), custom_call_target="tpu_custom_call" | custom-call | tf_op jit(solution)/shard_map/pallas_call | solution.py:436
  155.3 0.1 collective-permute-start.18
  155.4 0.0 collective-permute-done.19.refs_0_
  155.4 0.0 collective-permute-done.20.refs_1_
  155.4 7.5 %shard_map.138 = (bf16[192,2048]{1,0:T(8,128)(2,1)S(1)}, bf16[192,2048]{1,0:T(8,128)(2,1)S(1)}) custom-call(bf16[192,2048]{1,0:T(8,128)(2,1)S(1)} %collective-permute-done.19.refs_0_, bf16[192,2048]{1,0:T(8,128)(2,1)S(1)} %collective-permute-done.20.refs_1_, bf16[4224,2048]{1,0:T(8,128)(2,1)S(1)} %pack.1.refs_1_.refs_2_), custom_call_target="tpu_custom_call" | custom-call | tf_op jit(solution)/shard_map/pallas_call | solution.py:436
  162.9 1.2 collective-permute-start.21
  164.2 2.7 %collective-permute-start.22 = (bf16[192,2048]{1,0:T(8,128)(2,1)S(1)}, bf16[192,2048]{1,0:T(8,128)(2,1)S(1)}, u32[]{:S(2)}, u32[]{:S(2)}) collective-permute-start(bf16[192,2048]{1,0:T(8,128)(2,1)S(1)} %get-tuple-element.20), channel_id=1, source_target_pairs={{0,32},{1,97},{2,34},{3,99},{4,36},{5,101},{6,38},{7,103},{8,40},{... | collective-permute-start | bytes 2359304 | tf_op jit(solution)/shard_map/ppermute | solution.py:53
  166.8 5.1 %shard_map.136 = bf16[192,2048]{1,0:T(8,128)(2,1)S(1)} custom-call(bf16[192,2048]{1,0:T(8,128)(2,1)S(1)} %bitcast.19, bf16[4224,2048]{1,0:T(8,128)(2,1)S(1)} %pack.1.refs_1_.refs_2_), custom_call_target="tpu_custom_call" | custom-call | tf_op jit(solution)/shard_map/pallas_call | solution.py:436
  172.0 2.7 %collective-permute-done.21 = bf16[192,2048]{1,0:T(8,128)(2,1)S(1)} collective-permute-done((bf16[192,2048]{1,0:T(8,128)(2,1)S(1)}, bf16[192,2048]{1,0:T(8,128)(2,1)S(1)}, u32[]{:S(2)}, u32[]{:S(2)}) %collective-permute-start.21) | collective-permute-done | bytes 786464 | tf_op jit(solution)/shard_map/ppermute | solution.py:53
  174.7 2.4 %collective-permute-done.22 = bf16[192,2048]{1,0:T(8,128)(2,1)S(1)} collective-permute-done((bf16[192,2048]{1,0:T(8,128)(2,1)S(1)}, bf16[192,2048]{1,0:T(8,128)(2,1)S(1)}, u32[]{:S(2)}, u32[]{:S(2)}) %collective-permute-start.22) | collective-permute-done | bytes 786464 | tf_op jit(solution)/shard_map/ppermute | solution.py:53
  177.1 1.4 add_convert_fusion
  178.5 6.0 %all-to-all-start.1 = ((bf16[8,24,2048]{2,1,0:T(8,128)(2,1)}), bf16[8,24,2048]{2,1,0:T(8,128)(2,1)S(1)}, u32[]{:S(2)}, u32[]{:S(2)}) async-start(bf16[8,24,2048]{2,1,0:T(8,128)(2,1)} %bitcast.14), calls=%async_computation.1 | async-start | bytes 1572864 | tf_op jit(solution)/shard_map/all_to_all | solution.py:509
  184.4 0.4 weigh.1
  184.8 11.8 %all-to-all-done.1 = bf16[8,24,2048]{2,1,0:T(8,128)(2,1)S(1)} async-done(((bf16[8,24,2048]{2,1,0:T(8,128)(2,1)}), bf16[8,24,2048]{2,1,0:T(8,128)(2,1)S(1)}, u32[]{:S(2)}, u32[]{:S(2)}) %all-to-all-start.1) | async-done | bytes 786464 | tf_op jit(solution)/shard_map/all_to_all | solution.py:509
  196.6 1.1 finish.1
  (18 shorter events, 0.0 us)
Async XLA Ops:
  1.1 8.6 %collective-permute-start = (bf16[64,2176]{1,0:T(8,128)(2,1)S(1)}, bf16[64,2176]{1,0:T(8,128)(2,1)S(1)}, u32[]{:S(2)}, u32[]{:S(2)}) collective-permute-start(bf16[64,2176]{1,0:T(8,128)(2,1)S(1)} %prepare.1.c0), channel_id=1, source_target_pairs={{0,2},{1,7},{2,0},{3,5},{4,6},{5,3},{6,4},{7,1},{8,10},{9,15},{10,... | collective-permute-start | bytes 835592 | tf_op jit(solution)/shard_map/ppermute | solution.py:57
  5.8 85.2 %collective-permute-start.10 = (bf16[2,352,2048]{2,1,0:T(8,128)(2,1)}, bf16[2,352,2048]{2,1,0:T(8,128)(2,1)S(1)}, u32[]{:S(2)}, u32[]{:S(2)}) collective-permute-start(bf16[2,352,2048]{2,1,0:T(8,128)(2,1)} %bitcast.29), channel_id=1, source_target_pairs={{0,8},{1,25},{2,10},{3,27},{4,12},{5,29},{6,14},{7,31},{8,0},{9,17... | collective-permute-start | bytes 8650760 | tf_op jit(solution)/shard_map/ppermute | solution.py:53
  8.3 6.7 %collective-permute-start.1 = (bf16[64,2176]{1,0:T(8,128)(2,1)S(1)}, bf16[64,2176]{1,0:T(8,128)(2,1)S(1)}, u32[]{:S(2)}, u32[]{:S(2)}) collective-permute-start(bf16[64,2176]{1,0:T(8,128)(2,1)S(1)} %prepare.1.c0), channel_id=1, source_target_pairs={{0,6},{1,3},{2,4},{3,1},{4,2},{5,7},{6,0},{7,5},{8,14},{9,11},{10,... | collective-permute-start | bytes 835592 | tf_op jit(solution)/shard_map/ppermute | solution.py:57
  9.7 7.2 %collective-permute-start.2 = (bf16[64,2176]{1,0:T(8,128)(2,1)S(1)}, bf16[64,2176]{1,0:T(8,128)(2,1)S(1)}, u32[]{:S(2)}, u32[]{:S(2)}) collective-permute-start(bf16[64,2176]{1,0:T(8,128)(2,1)S(1)} %collective-permute-done.c1), channel_id=1, source_target_pairs={{0,6},{1,3},{2,4},{3,1},{4,2},{5,7},{6,0},{7,5},{8,14},{9,11},{10,... | collective-permute-start | bytes 835592 | tf_op jit(solution)/shard_map/ppermute | solution.py:57
  9.7 10.7 %collective-permute-start.3 = (bf16[64,2176]{1,0:T(8,128)(2,1)S(1)}, bf16[64,2176]{1,0:T(8,128)(2,1)S(1)}, u32[]{:S(2)}, u32[]{:S(2)}) collective-permute-start(bf16[64,2176]{1,0:T(8,128)(2,1)S(1)} %prepare.1.c0), channel_id=1, source_target_pairs={{0,1},{1,0},{2,3},{3,2},{4,5},{5,4},{6,7},{7,6},{8,9},{9,8},{10,11... | collective-permute-start | bytes 835592 | tf_op jit(solution)/shard_map/ppermute | solution.py:57
  14.9 5.6 %collective-permute-start.4 = (bf16[64,2176]{1,0:T(8,128)(2,1)S(1)}, bf16[64,2176]{1,0:T(8,128)(2,1)S(1)}, u32[]{:S(2)}, u32[]{:S(2)}) collective-permute-start(bf16[64,2176]{1,0:T(8,128)(2,1)S(1)} %collective-permute-done.c1), channel_id=1, source_target_pairs={{0,1},{1,0},{2,3},{3,2},{4,5},{5,4},{6,7},{7,6},{8,9},{9,8},{10,11... | collective-permute-start | bytes 835592 | tf_op jit(solution)/shard_map/ppermute | solution.py:57
  14.9 5.5 %collective-permute-start.5 = (bf16[64,2176]{1,0:T(8,128)(2,1)S(1)}, bf16[64,2176]{1,0:T(8,128)(2,1)S(1)}, u32[]{:S(2)}, u32[]{:S(2)}) collective-permute-start(bf16[64,2176]{1,0:T(8,128)(2,1)S(1)} %collective-permute-done.1.c2), channel_id=1, source_target_pairs={{0,1},{1,0},{2,3},{3,2},{4,5},{5,4},{6,7},{7,6},{8,9},{9,8},{10,11... | collective-permute-start | bytes 835592 | tf_op jit(solution)/shard_map/ppermute | solution.py:57
  16.9 3.6 %collective-permute-start.6 = (bf16[64,2176]{1,0:T(8,128)(2,1)S(1)}, bf16[64,2176]{1,0:T(8,128)(2,1)S(1)}, u32[]{:S(2)}, u32[]{:S(2)}) collective-permute-start(bf16[64,2176]{1,0:T(8,128)(2,1)S(1)} %collective-permute-done.2.c3), channel_id=1, source_target_pairs={{0,1},{1,0},{2,3},{3,2},{4,5},{5,4},{6,7},{7,6},{8,9},{9,8},{10,11... | collective-permute-start | bytes 835592 | tf_op jit(solution)/shard_map/ppermute | solution.py:57
  20.6 18.3 %copy-start.6 = (bf16[1,2048,2,352]{1,3,2,0:T(8,128)(2,1)S(1)}, bf16[1,2048,2,352]{1,3,2,0:T(8,128)(2,1)}, u32[]{:S(2)}) copy-start(bf16[1,2048,2,352]{1,3,2,0:T(8,128)(2,1)} %param.26) | copy-start | bytes 8650756
  20.6 19.6 %copy-start.7 = (bf16[1,352,2048]{2,1,0:T(8,128)(2,1)S(1)}, bf16[1,352,2048]{2,1,0:T(8,128)(2,1)}, u32[]{:S(2)}) copy-start(bf16[1,352,2048]{2,1,0:T(8,128)(2,1)} %param.27) | copy-start | bytes 4325380
  38.4 2.7 %collective-permute-start.7 = (bf16[256,2048]{1,0:T(8,128)(2,1)S(1)}, bf16[256,2048]{1,0:T(8,128)(2,1)S(1)}, u32[]{:S(2)}, u32[]{:S(2)}) collective-permute-start(bf16[256,2048]{1,0:T(8,128)(2,1)S(1)} %get-tuple-element.14), channel_id=1, source_target_pairs={{0,1},{1,0},{2,3},{3,2},{4,5},{5,4},{6,7},{7,6},{8,9},{9,8},{10,11... | collective-permute-start | bytes 3145736 | tf_op jit(solution)/shard_map/ppermute | solution.py:57
  38.9 84.8 %collective-permute-start.11 = (bf16[2,352,2048]{2,1,0:T(8,128)(2,1)S(1)}, bf16[2,352,2048]{2,1,0:T(8,128)(2,1)S(1)}, u32[]{:S(2)}, u32[]{:S(2)}) collective-permute-start(bf16[2,352,2048]{2,1,0:T(8,128)(2,1)S(1)} %bitcast.31), channel_id=1, source_target_pairs={{0,96},{1,33},{2,98},{3,35},{4,100},{5,37},{6,102},{7,39},{8,104},... | collective-permute-start | bytes 8650760 | tf_op jit(solution)/shard_map/ppermute | solution.py:53
  40.2 47.8 %collective-permute-start.15 = (bf16[352,2048]{1,0:T(8,128)(2,1)S(1)}, bf16[352,2048]{1,0:T(8,128)(2,1)S(1)}, u32[]{:S(2)}, u32[]{:S(2)}) collective-permute-start(bf16[352,2048]{1,0:T(8,128)(2,1)S(1)} %bitcast.33), channel_id=1, source_target_pairs={{0,96},{1,33},{2,98},{3,35},{4,100},{5,37},{6,102},{7,39},{8,104},... | collective-permute-start | bytes 4325384 | tf_op jit(solution)/shard_map/ppermute | solution.py:53
  41.3 52.6 %collective-permute-start.8 = (bf16[128,2048]{1,0:T(8,128)(2,1)S(1)}, bf16[128,2048]{1,0:T(8,128)(2,1)S(1)}, u32[]{:S(2)}, u32[]{:S(2)}) collective-permute-start(bf16[128,2048]{1,0:T(8,128)(2,1)S(1)} %add_convert_fusion.1), channel_id=1, source_target_pairs={{0,2},{1,7},{2,0},{3,5},{4,6},{5,3},{6,4},{7,1},{8,10},{9,15},{10,... | collective-permute-start | bytes 1572872 | tf_op jit(solution)/shard_map/ppermute | solution.py:57
  44.3 78.2 %collective-permute-start.14 = (bf16[352,2048]{1,0:T(8,128)(2,1)S(1)}, bf16[352,2048]{1,0:T(8,128)(2,1)S(1)}, u32[]{:S(2)}, u32[]{:S(2)}) collective-permute-start(bf16[352,2048]{1,0:T(8,128)(2,1)S(1)} %bitcast.34), channel_id=1, source_target_pairs={{0,8},{1,25},{2,10},{3,27},{4,12},{5,29},{6,14},{7,31},{8,0},{9,17... | collective-permute-start | bytes 4325384 | tf_op jit(solution)/shard_map/ppermute | solution.py:53
  87.9 38.5 %collective-permute-start.16 = (bf16[352,2048]{1,0:T(8,128)(2,1)S(1)}, bf16[352,2048]{1,0:T(8,128)(2,1)S(1)}, u32[]{:S(2)}, u32[]{:S(2)}) collective-permute-start(bf16[352,2048]{1,0:T(8,128)(2,1)S(1)} %collective-permute-done.15.refs_7_), channel_id=1, source_target_pairs={{0,8},{1,25},{2,10},{3,27},{4,12},{5,29},{6,14},{7,31},{8,0},{9,17... | collective-permute-start | bytes 4325384 | tf_op jit(solution)/shard_map/ppermute | solution.py:53
  91.0 1.6 copy-start.4
  91.0 8.8 %copy-start = (bf16[64,2048]{1,0:T(8,128)(2,1)S(1)}, bf16[64,2048]{1,0:T(8,128)(2,1)}, u32[]{:S(2)}) copy-start(bf16[64,2048]{1,0:T(8,128)(2,1)} %hidden.3) | copy-start | bytes 786436
  91.0 8.8 %copy-start.2 = (f32[2048]{0:T(1024)S(1)}, f32[2048]{0:T(1024)}, u32[]{:S(2)}) copy-start(f32[2048]{0:T(1024)} %param.24) | copy-start | bytes 24580
  91.0 8.7 %copy-start.3 = (s32[64,2]{0,1:T(2,128)S(1)}, s32[64,2]{0,1:T(2,128)}, u32[]{:S(2)}) copy-start(s32[64,2]{0,1:T(2,128)} %param.17) | copy-start | bytes 1540
  92.6 53.3 %collective-permute-start.12 = (bf16[528,2048]{1,0:T(8,128)(2,1)S(1)}, bf16[528,2048]{1,0:T(8,128)(2,1)S(1)}, u32[]{:S(2)}, u32[]{:S(2)}) collective-permute-start(bf16[528,2048]{1,0:T(8,128)(2,1)S(1)} %slice.31), channel_id=1, source_target_pairs={{0,96},{1,33},{2,98},{3,35},{4,100},{5,37},{6,102},{7,39},{8,104},... | collective-permute-start | bytes 6488072 | tf_op jit(solution)/shard_map/ppermute | solution.py:53
  94.0 5.8 %collective-permute-start.9 = (bf16[64,2048]{1,0:T(8,128)(2,1)S(1)}, bf16[64,2048]{1,0:T(8,128)(2,1)S(1)}, u32[]{:S(2)}, u32[]{:S(2)}) collective-permute-start(bf16[64,2048]{1,0:T(8,128)(2,1)S(1)} %add_convert_fusion.2), channel_id=1, source_target_pairs={{0,6},{1,3},{2,4},{3,1},{4,2},{5,7},{6,0},{7,5},{8,14},{9,11},{10,... | collective-permute-start | bytes 786440 | tf_op jit(solution)/shard_map/ppermute | solution.py:57
  122.5 27.7 %collective-permute-start.17 = (bf16[192,2048]{1,0:T(8,128)(2,1)S(1)}, bf16[192,2048]{1,0:T(8,128)(2,1)S(1)}, u32[]{:S(2)}, u32[]{:S(2)}) collective-permute-start(bf16[192,2048]{1,0:T(8,128)(2,1)S(1)} %bitcast.16), channel_id=1, source_target_pairs={{0,56},{1,105},{2,58},{3,107},{4,60},{5,109},{6,62},{7,111},{8,48}... | collective-permute-start | bytes 2359304 | tf_op jit(solution)/shard_map/ppermute | solution.py:53
  122.5 32.9 %collective-permute-start.19 = (bf16[192,2048]{1,0:T(8,128)(2,1)S(1)}, bf16[192,2048]{1,0:T(8,128)(2,1)S(1)}, u32[]{:S(2)}, u32[]{:S(2)}) collective-permute-start(bf16[192,2048]{1,0:T(8,128)(2,1)S(1)} %bitcast.17), channel_id=1, source_target_pairs={{0,24},{1,9},{2,26},{3,11},{4,28},{5,13},{6,30},{7,15},{8,16},{9,1... | collective-permute-start | bytes 2359304 | tf_op jit(solution)/shard_map/ppermute | solution.py:53
  123.6 22.3 %copy-start.5 = (bf16[2,352,2048]{2,1,0:T(8,128)(2,1)}, bf16[2,352,2048]{2,1,0:T(8,128)(2,1)S(1)}, u32[]{:S(2)}) copy-start(bf16[2,352,2048]{2,1,0:T(8,128)(2,1)S(1)} %collective-permute-done.11.refs_2_) | copy-start | bytes 8650756
  123.6 31.8 %collective-permute-start.20 = (bf16[192,2048]{1,0:T(8,128)(2,1)S(1)}, bf16[192,2048]{1,0:T(8,128)(2,1)S(1)}, u32[]{:S(2)}, u32[]{:S(2)}) collective-permute-start(bf16[192,2048]{1,0:T(8,128)(2,1)S(1)} %bitcast.18), channel_id=1, source_target_pairs={{0,32},{1,97},{2,34},{3,99},{4,36},{5,101},{6,38},{7,103},{8,40},{... | collective-permute-start | bytes 2359304 | tf_op jit(solution)/shard_map/ppermute | solution.py:53
  126.4 19.4 %collective-permute-start.13 = (bf16[176,2048]{1,0:T(8,128)(2,1)S(1)}, bf16[176,2048]{1,0:T(8,128)(2,1)S(1)}, u32[]{:S(2)}, u32[]{:S(2)}) collective-permute-start(bf16[176,2048]{1,0:T(8,128)(2,1)S(1)} %slice.32), channel_id=1, source_target_pairs={{0,8},{1,25},{2,10},{3,27},{4,12},{5,29},{6,14},{7,31},{8,0},{9,17... | collective-permute-start | bytes 2162696 | tf_op jit(solution)/shard_map/ppermute | solution.py:53
  155.3 16.7 %collective-permute-start.18 = (bf16[192,2048]{1,0:T(8,128)(2,1)S(1)}, bf16[192,2048]{1,0:T(8,128)(2,1)S(1)}, u32[]{:S(2)}, u32[]{:S(2)}) collective-permute-start(bf16[192,2048]{1,0:T(8,128)(2,1)S(1)} %shard_map.137), channel_id=1, source_target_pairs={{0,56},{1,105},{2,58},{3,107},{4,60},{5,109},{6,62},{7,111},{8,48}... | collective-permute-start | bytes 2359304 | tf_op jit(solution)/shard_map/ppermute | solution.py:53
  162.9 11.7 %collective-permute-start.21 = (bf16[192,2048]{1,0:T(8,128)(2,1)S(1)}, bf16[192,2048]{1,0:T(8,128)(2,1)S(1)}, u32[]{:S(2)}, u32[]{:S(2)}) collective-permute-start(bf16[192,2048]{1,0:T(8,128)(2,1)S(1)} %get-tuple-element.19), channel_id=1, source_target_pairs={{0,24},{1,9},{2,26},{3,11},{4,28},{5,13},{6,30},{7,15},{8,16},{9,1... | collective-permute-start | bytes 2359304 | tf_op jit(solution)/shard_map/ppermute | solution.py:53
  164.2 12.9 %collective-permute-start.22 = (bf16[192,2048]{1,0:T(8,128)(2,1)S(1)}, bf16[192,2048]{1,0:T(8,128)(2,1)S(1)}, u32[]{:S(2)}, u32[]{:S(2)}) collective-permute-start(bf16[192,2048]{1,0:T(8,128)(2,1)S(1)} %get-tuple-element.20), channel_id=1, source_target_pairs={{0,32},{1,97},{2,34},{3,99},{4,36},{5,101},{6,38},{7,103},{8,40},{... | collective-permute-start | bytes 2359304 | tf_op jit(solution)/shard_map/ppermute | solution.py:53
  178.5 6.0 %copy-start.1 = (f32[2048,8]{0,1:T(8,128)S(1)}, f32[2048,8]{0,1:T(8,128)}, u32[]{:S(2)}) copy-start(f32[2048,8]{0,1:T(8,128)} %param.25) | copy-start | bytes 196612
  178.5 18.1 %all-to-all-start.1 = ((bf16[8,24,2048]{2,1,0:T(8,128)(2,1)}), bf16[8,24,2048]{2,1,0:T(8,128)(2,1)S(1)}, u32[]{:S(2)}, u32[]{:S(2)}) async-start(bf16[8,24,2048]{2,1,0:T(8,128)(2,1)} %bitcast.14), calls=%async_computation.1 | async-start | bytes 1572864 | tf_op jit(solution)/shard_map/all_to_all | solution.py:509
